TPU v7x, 32 devices: a whole 2x2x4 slice. The times are simulated.
32 devices in a mesh: section: 8 (over z, x), tp: 4 (over y, core).
Axes of the slice: x: 2, y: 2, z: 4, core: 2. Of those that a mesh axis runs over, the one named last changes fastest.
Arguments:
- x_handed: bfloat16 [8, 768, 4096], P('section', None, 'tp'), may hold values from -6 to 6
- cot_handed: bfloat16 [8, 768, 4096], P('section', None, 'tp'), may hold values from -6 to 6
- w_query: bfloat16 [8, 4096, 4096], P('section', None, 'tp'), may hold values from -0.1875 to 0.1875
- key_value_weight: bfloat16 [8, 4096, 1024], P('section', None, 'tp'), may hold values from -0.125 to 0.125
- w_out: bfloat16 [8, 4096, 4096], P('section', 'tp'), may hold values from -0.1875 to 0.1875
- norm_gain: float32 [8, 4096], P('section'), may hold values from 0.1 to 1.9
Outputs:
- layer_out: bfloat16 [8, 768, 4096], P('section', None, 'tp')
- grad_in: bfloat16 [8, 768, 4096], P('section', None, 'tp')
- grad_query: bfloat16 [8, 4096, 4096], P('section', None, 'tp')
- grad_keyval: bfloat16 [8, 4096, 1024], P('section', None, 'tp')
- grad_out: bfloat16 [8, 4096, 4096], P('section', 'tp')
- grad_gain: float32 [8, 4096], P('section')
All inputs are finite; a program needn't handle non-finite values.
Results may differ from a plain program's by a relative error of at most 0.03.
Values may be sent and summed in bfloat16 or wider, within the bound.
A program may use at most 128 MiB of HBM per device.

v0:
```python
import jax
import jax.numpy as jnp
from jax import lax
from jax.sharding import PartitionSpec as P

HEAD_SIZE = 128
QUERY_HEADS = 32
KEY_VALUE_HEADS = 4


def shifted(value, axis, steps):
    count = lax.axis_size(axis)
    pairs = [(source, (source + steps) % count) for source in range(count)]
    return lax.ppermute(value, axis, pairs)


def on_device(x_handed, cot_handed, w_query, key_value_weight, w_out, norm_gain):
    x_part = shifted(x_handed, "section", 1)[0]
    dy_part = shifted(cot_handed, "section", -1)[0]
    wq_dev = w_query[0]
    wkv_dev = key_value_weight[0]
    wo_dev = w_out[0]
    gain_row = norm_gain[0]
    heads_per_device = wq_dev.shape[1] // HEAD_SIZE
    score_scale = HEAD_SIZE ** (-0.5)
    x_all = lax.all_gather(x_part, "tp", axis=1, tiled=True)
    sequence_length = x_all.shape[0]
    tok_rows = sequence_length // lax.axis_size("tp")
    row_start = lax.axis_index("tp") * tok_rows
    x_float = x_all.astype(jnp.float32)
    inv_rms = lax.rsqrt(jnp.mean(x_float * x_float, axis=-1, keepdims=True) + 1e-05)
    unit_x = x_float * inv_rms
    normed_all = (unit_x * gain_row).astype(jnp.bfloat16)
    queries = jnp.dot(normed_all, wq_dev, preferred_element_type=jnp.float32).astype(jnp.bfloat16)
    kv_part = jnp.dot(normed_all, wkv_dev, preferred_element_type=jnp.float32).astype(jnp.bfloat16)
    key_value_pairs = lax.all_gather(kv_part, "tp", axis=1, tiled=True)
    key_value_head = lax.axis_index("tp") * heads_per_device // (QUERY_HEADS // KEY_VALUE_HEADS)
    key_rows = lax.dynamic_slice_in_dim(key_value_pairs, key_value_head * HEAD_SIZE, HEAD_SIZE, 1)
    value_rows_full = lax.dynamic_slice_in_dim(
        key_value_pairs, KEY_VALUE_HEADS * HEAD_SIZE + key_value_head * HEAD_SIZE, HEAD_SIZE, 1
    )
    query_heads = queries.reshape(sequence_length, heads_per_device, HEAD_SIZE)
    scores = (
        jnp.einsum("shd,td->hst", query_heads, key_rows, preferred_element_type=jnp.float32)
        * score_scale
    )
    row_ids = lax.broadcasted_iota(jnp.int32, (sequence_length, sequence_length), 0)
    col_ids = lax.broadcasted_iota(jnp.int32, (sequence_length, sequence_length), 1)
    causal = row_ids >= col_ids
    scores = jnp.where(causal[None], scores, jnp.float32(-1e30))
    row_max = jnp.max(scores, axis=-1, keepdims=True)
    shifted_exp = jnp.exp(scores - row_max)
    attn_probs = shifted_exp / jnp.sum(shifted_exp, axis=-1, keepdims=True)
    probs_bf = attn_probs.astype(jnp.bfloat16)
    attended = jnp.einsum(
        "hst,td->shd", probs_bf, value_rows_full, preferred_element_type=jnp.float32
    ).astype(jnp.bfloat16)
    attn_flat = attended.reshape(sequence_length, heads_per_device * HEAD_SIZE)
    out_terms = jnp.dot(attn_flat, wo_dev, preferred_element_type=jnp.float32)
    mixed_part = lax.psum_scatter(
        out_terms.astype(jnp.bfloat16), "tp", scatter_dimension=1, tiled=True
    ).astype(jnp.float32)
    layer_out = (x_part.astype(jnp.float32) + mixed_part).astype(jnp.bfloat16)
    dy_all = lax.all_gather(dy_part, "tp", axis=1, tiled=True)
    grad_out = jnp.einsum(
        "sk,sd->kd", attn_flat, dy_all, preferred_element_type=jnp.float32
    ).astype(jnp.bfloat16)
    d_attended = jnp.einsum("sd,kd->sk", dy_all, wo_dev, preferred_element_type=jnp.float32).astype(
        jnp.bfloat16
    )
    d_att_heads = d_attended.reshape(sequence_length, heads_per_device, HEAD_SIZE)
    d_probs = jnp.einsum(
        "shd,td->hst", d_att_heads, value_rows_full, preferred_element_type=jnp.float32
    )
    row_delta = jnp.einsum(
        "shd,shd->hs", d_att_heads.astype(jnp.float32), attended.astype(jnp.float32)
    )
    d_scores = (attn_probs * (d_probs - row_delta[:, :, None]) * score_scale).astype(jnp.bfloat16)
    d_queries = jnp.einsum("hst,td->shd", d_scores, key_rows, preferred_element_type=jnp.float32)
    d_queries = d_queries.astype(jnp.bfloat16).reshape(
        sequence_length, heads_per_device * HEAD_SIZE
    )
    d_key_rows = jnp.einsum(
        "hst,shd->td", d_scores, query_heads, preferred_element_type=jnp.float32
    )
    value_row_gradient = jnp.einsum(
        "hst,shd->td", probs_bf, d_att_heads, preferred_element_type=jnp.float32
    )
    key_value_contribution = jnp.zeros(
        (sequence_length, 2 * KEY_VALUE_HEADS * HEAD_SIZE), jnp.float32
    )
    key_value_contribution = lax.dynamic_update_slice(
        key_value_contribution, d_key_rows, (jnp.int32(0), key_value_head * HEAD_SIZE)
    )
    key_value_contribution = lax.dynamic_update_slice(
        key_value_contribution,
        value_row_gradient,
        (jnp.int32(0), KEY_VALUE_HEADS * HEAD_SIZE + key_value_head * HEAD_SIZE),
    )
    d_keyvals = lax.psum_scatter(
        key_value_contribution.astype(jnp.bfloat16), "tp", scatter_dimension=1, tiled=True
    )
    grad_query = jnp.einsum(
        "sd,sk->dk", normed_all, d_queries, preferred_element_type=jnp.float32
    ).astype(jnp.bfloat16)
    grad_keyval = jnp.einsum(
        "sd,sk->dk", normed_all, d_keyvals, preferred_element_type=jnp.float32
    ).astype(jnp.bfloat16)
    from_query = jnp.einsum("sk,dk->sd", d_queries, wq_dev, preferred_element_type=jnp.float32)
    from_keyval = jnp.einsum("sk,dk->sd", d_keyvals, wkv_dev, preferred_element_type=jnp.float32)
    d_normed = lax.psum_scatter(
        (from_query + from_keyval).astype(jnp.bfloat16), "tp", scatter_dimension=0, tiled=True
    ).astype(jnp.float32)
    unit_rows = lax.dynamic_slice_in_dim(unit_x, row_start, tok_rows, 0)
    inv_rows = lax.dynamic_slice_in_dim(inv_rms, row_start, tok_rows, 0)
    dy_rows = lax.dynamic_slice_in_dim(dy_all, row_start, tok_rows, 0).astype(jnp.float32)
    gain_local = jnp.sum(d_normed * unit_rows, axis=0)
    grad_gain = lax.psum(gain_local, "tp")
    d_unit = d_normed * gain_row
    d_input = inv_rows * (d_unit - unit_rows * jnp.mean(d_unit * unit_rows, axis=-1, keepdims=True))
    grad_rows = (dy_rows + d_input).astype(jnp.bfloat16)
    grad_in = lax.all_to_all(grad_rows, "tp", split_axis=1, concat_axis=0, tiled=True)
    return (
        layer_out[None],
        grad_in[None],
        grad_query[None],
        grad_keyval[None],
        grad_out[None],
        grad_gain[None],
    )


def solution(mesh):
    return jax.shard_map(
        on_device,
        mesh=mesh,
        in_specs=(
            P("section", None, "tp"),
            P("section", None, "tp"),
            P("section", None, "tp"),
            P("section", None, "tp"),
            P("section", "tp", None),
            P("section", None),
        ),
        out_specs=(
            P("section", None, "tp"),
            P("section", None, "tp"),
            P("section", None, "tp"),
            P("section", None, "tp"),
            P("section", "tp", None),
            P("section", None),
        ),
        check_vma=False,
    )
```

profile of v0, /device:TPU:0, one launch (start us, length us, event | category | flops | bytes accessed | tf_op | source)
XLA Modules:
  0.0 405.7 jit_solution(3061922801894972612)
XLA Ops:
  7.2 0.0 copy-start
  7.2 0.0 copy-start.8
  7.2 0.0 all-gather.8.cloned.1.call-start
  7.2 3.0 collective-permute-start
  10.2 37.7 %collective-permute-done = bf16[1,768,1024]{2,1,0:T(8,128)(2,1)} collective-permute-done((bf16[1,768,1024]{2,1,0:T(8,128)(2,1)}, bf16[1,768,1024]{2,1,0:T(8,128)(2,1)}, u32[]{:S(2)}, u32[]{:S(2)}) %collective-permute-start) | collective-permute-done | bytes 1572896 | tf_op jit(solution)/shard_map/ppermute | solution.py:14
  48.0 0.0 all-gather.8.cloned.1.call-update
  48.0 0.0 all-gather.10.cloned.1.call-start
  48.1 1.8 collective-permute-start.1
  49.8 34.2 %collective-permute-done.1 = bf16[1,768,1024]{2,1,0:T(8,128)(2,1)} collective-permute-done((bf16[1,768,1024]{2,1,0:T(8,128)(2,1)}, bf16[1,768,1024]{2,1,0:T(8,128)(2,1)}, u32[]{:S(2)}, u32[]{:S(2)}) %collective-permute-start.1) | collective-permute-done | bytes 1572896 | tf_op jit(solution)/shard_map/ppermute | solution.py:14
  84.0 0.0 all-gather.10.cloned.1.call-update
  84.0 0.0 all-gather.6.cloned.1.call-start
  84.1 0.2 iota_compare_fusion
  84.3 8.7 %all-gather.8.cloned.1.call-done = bf16[1,768,4096]{2,1,0:T(8,128)(2,1)} async-done(((bf16[1,768,1024]{2,1,0:T(8,128)(2,1)}), bf16[1,768,4096]{2,1,0:T(8,128)(2,1)}) %all-gather.8.cloned.1.call-update) | async-done | bytes 6291472 | tf_op jit(solution)/shard_map/all_gather | solution.py:26
  93.0 4.2 %fusion.5 = f32[768]{0:T(1024)S(1)} fusion(bf16[1,768,4096]{2,1,0:T(8,128)(2,1)} %all-gather.8.cloned.1.call-done), kind=kLoop, calls=%fused_computation.10 | loop fusion | flops 9436416 | bytes 6294528 | tf_op jit(solution)/shard_map/reduce_sum | solution.py:31
  97.2 0.0 copy-done
  97.2 0.0 copy-done.8
  97.3 0.3 copy-done.1
  97.6 2.6 fusion.63
  100.3 0.0 all-gather.6.cloned.1.call-update
  100.3 0.2 reduce-scatter.6.cloned.1.call-start
  100.5 40.5 %all-gather.10.cloned.1.call-done = bf16[1,768,4096]{2,1,0:T(8,128)(2,1)} async-done(((bf16[1,768,1024]{2,1,0:T(8,128)(2,1)}), bf16[1,768,4096]{2,1,0:T(8,128)(2,1)}) %all-gather.10.cloned.1.call-update) | async-done | bytes 6291472 | tf_op jit(solution)/shard_map/all_gather | solution.py:64
  141.0 11.0 %fusion.40 = bf16[768,1024]{1,0:T(8,128)(2,1)S(1)} fusion(bf16[1,1024,4096]{2,1,0:T(8,128)(2,1)} %param.10, bf16[1,768,4096]{2,1,0:T(8,128)(2,1)} %all-gather.10.cloned.1.call-done), kind=kOutput, calls=%fused_computation.51 | convolution fusion | flops 6443237376 | bytes 16252928 | tf_op jit(solution)/shard_map/sd,kd->sk/dot_general | solution.py:68
  152.0 0.0 copy-start.3
  152.0 1.1 copy-done.3
  153.1 0.4 copy.45
  153.6 2.0 bitcast_convert_fusion
  155.5 3.5 copy.37
  159.1 12.4 %fusion.58 = bf16[96,8,8,128]{3,2,1,0:T(8,128)(2,1)} fusion(bf16[1,4096,1024]{2,1,0:T(8,128)(2,1)} %param.8, f32[4096]{0:T(1024)S(1)} %bitcast.183, f32[768]{0:T(1024)S(1)} %add_rsqrt_fusion, bf16[1,768,4096]{2,1,0:T(8,128)(2,1)} %all-gather.8.cloned.1.call-done), kind=kOutput, calls=%fused_computation.65 | convolution fusion | flops 6455820288 | bytes 16272384 | tf_op jit(solution)/shard_map/dot_general | solution.py:34
  171.4 11.6 %fusion.106 = (f32[8,768]{1,0:T(8,128)S(1)}, f32[8,768,768]{1,2,0:T(8,128)}) fusion(pred[768,768]{0,1:T(8,128)(4,1)S(1)} %iota_compare_fusion, bf16[96,8,8,128]{3,2,1,0:T(8,128)(2,1)} %fusion.58, bf16[768,1024]{1,0:T(8,128)(2,1)} %all-gather.6.cloned.1.call-done, s32[]{:T(128)S(6)} %select_n.24), kind=kOutput, calls=%fused_computation.95 | convolution fusion | flops 1226834688 | bytes 21258244 | tf_op jit(solution)/shard_map/sub | solution.py:52
  183.1 7.5 %fusion.17 = bf16[8,768,768]{1,2,0:T(8,128)(2,1)S(1)} fusion(f32[8,768,768]{1,2,0:T(8,128)} %get-tuple-element.9, f32[8,768]{1,0:T(8,128)S(1)} %get-tuple-element.8), kind=kLoop, calls=%fused_computation.27 | loop fusion | flops 9437184 | bytes 28336128 | tf_op jit(solution)/shard_map/convert_element_type | solution.py:54
  190.6 0.0 copy-start.4
  190.6 3.9 multiply_reduce_fusion
  194.5 0.0 copy-done.4
  194.5 10.5 %fusion.3 = bf16[8,768,768]{1,2,0:T(8,128)(2,1)} fusion(f32[8,768]{1,0:T(8,128)S(1)} %get-tuple-element.10, f32[8,768,768]{1,2,0:T(8,128)} %get-tuple-element.9, f32[8,768]{1,0:T(8,128)S(1)} %get-tuple-element.8, bf16[768,1024]{1,0:T(8,128)(2,1)} %all-gather.6.cloned.1.call-done, s32[]{:T(128)S(6)} %select_n.23, bf16[768,1024]{1,0:T(8,128)(2,1)S(1)} %copy-done.4), kind=kOutput, calls=%fused_computation.4 | convolution fusion | flops 1231552512 | bytes 30130180 | tf_op jit(solution)/shard_map/shd,td->hst/dot_general | solution.py:72
  205.0 1.3 broadcast_in_dim.42
  206.3 7.5 %fusion.69 = bf16[768,1024]{1,0:T(8,128)(2,1)} fusion(bf16[768,1024]{1,0:T(8,128)(2,1)} %broadcast_in_dim.42, s32[]{:T(128)S(6)} %select_n.24, bf16[8,768,768]{1,2,0:T(8,128)(2,1)} %fusion.3, bf16[96,8,8,128]{3,2,1,0:T(8,128)(2,1)} %fusion.58), kind=kOutput, calls=%fused_computation.70 | convolution fusion | flops 1207959552 | bytes 11403268 | tf_op jit(solution)/shard_map/hst,shd->td/dot_general | solution.py:83
  213.8 3.3 fusion.75
  217.0 0.0 reduce-scatter.6.cloned.1.call-update
  217.1 0.0 reduce-scatter.8.cloned.1.call-start
  217.1 5.2 %convolution_convert_fusion.1 = bf16[128,8,768]{2,0,1:T(8,128)(2,1)S(1)} fusion(bf16[8,768,768]{1,2,0:T(8,128)(2,1)} %fusion.3, bf16[768,1024]{1,0:T(8,128)(2,1)} %all-gather.6.cloned.1.call-done, s32[]{:T(128)S(6)} %select_n.24), kind=kOutput, calls=%fused_computation.52 | convolution fusion | flops 1208745984 | bytes 11206660 | tf_op jit(solution)/shard_map/hst,td->shd/dot_general | solution.py:79
  222.4 0.0 copy-start.5
  222.4 1.1 copy-done.5
  223.5 13.2 %fusion.13 = f32[768,4096]{1,0:T(8,128)} fusion(bf16[768,1024]{0,1:T(8,128)(2,1)S(1)} %bitcast.180, bf16[1,4096,1024]{2,1,0:T(8,128)(2,1)} %param.8), kind=kOutput, calls=%fused_computation.21 | convolution fusion | flops 6442450944 | bytes 22544384 | tf_op jit(solution)/shard_map/sk,dk->sd/dot_general | solution.py:109
  236.7 8.7 %reduce-scatter.6.cloned.1.call-done = bf16[768,256]{1,0:T(8,128)(2,1)} async-done(((bf16[768,1024]{1,0:T(8,128)(2,1)}), bf16[768,256]{1,0:T(8,128)(2,1)}) %reduce-scatter.6.cloned.1.call-update) | async-done | bytes 393232 | tf_op jit(solution)/shard_map/reduce_scatter | solution.py:100
  245.4 9.3 %add_convert_fusion = bf16[768,4096]{1,0:T(8,128)(2,1)} fusion(f32[768,4096]{1,0:T(8,128)} %fusion.13, bf16[768,256]{1,0:T(8,128)(2,1)} %reduce-scatter.6.cloned.1.call-done, bf16[1,4096,256]{2,1,0:T(8,128)(2,1)S(1)} %copy-done), kind=kOutput, calls=%fused_computation.11 | convolution fusion | flops 1616904192 | bytes 21364736 | tf_op jit(solution)/shard_map/sk,dk->sd/dot_general | solution.py:110
  254.6 0.0 reduce-scatter.8.cloned.1.call-update
  254.7 0.0 reduce-scatter.4.cloned.1.call-start
  254.7 11.8 %fusion.20 = bf16[768,4096]{1,0:T(8,128)(2,1)} fusion(bf16[768,1024]{0,1:T(8,128)(2,1)} %bitcast.177, bf16[1,1024,4096]{2,1,0:T(8,128)(2,1)} %param.10), kind=kOutput, calls=%fused_computation.29 | convolution fusion | flops 6445596672 | bytes 16252928 | tf_op jit(solution)/shard_map/dot_general | solution.py:59
  266.5 0.0 reduce-scatter.4.cloned.1.call-update
  266.5 0.1 dynamic-slice.3
  266.6 10.3 %convert_multiply_fusion = f32[768,4096]{1,0:T(8,128)} fusion(bf16[1,768,4096]{2,1,0:T(8,128)(2,1)} %all-gather.8.cloned.1.call-done, f32[768]{0:T(1024)S(1)} %add_rsqrt_fusion), kind=kLoop, calls=%fused_computation.7 | loop fusion | flops 6291456 | bytes 18877440 | tf_op jit(solution)/shard_map/mul | solution.py:32
  276.9 12.7 %convert_bitcast_fusion.1 = bf16[1,4096,1024]{2,1,0:T(8,128)(2,1)} fusion(bf16[768,1024]{0,1:T(8,128)(2,1)S(1)} %bitcast.181, f32[4096]{0:T(1024)S(1)} %bitcast.184, f32[768]{0:T(1024)S(1)} %add_rsqrt_fusion, bf16[1,768,4096]{2,1,0:T(8,128)(2,1)} %all-gather.8.cloned.1.call-done), kind=kOutput, calls=%fused_computation.26 | convolution fusion | flops 6459228160 | bytes 16272384 | tf_op jit(solution)/shard_map/sd,sk->dk/dot_general | solution.py:103
  289.6 23.6 %reduce-scatter.8.cloned.1.call-done = bf16[192,4096]{1,0:T(8,128)(2,1)} async-done(((bf16[768,4096]{1,0:T(8,128)(2,1)}), bf16[192,4096]{1,0:T(8,128)(2,1)}) %reduce-scatter.8.cloned.1.call-update) | async-done | bytes 1572880 | tf_op jit(solution)/shard_map/reduce_scatter | solution.py:111
  313.2 3.3 fusion.32
  316.5 3.8 fusion.31
  320.3 1.3 copy.79
  321.6 4.6 %all-to-all-start = ((bf16[192,4,1024]{2,0,1:T(8,128)(2,1)}), bf16[192,4,1024]{2,0,1:T(8,128)(2,1)}, u32[]{:S(2)}, u32[]{:S(2)}) async-start(bf16[192,4,1024]{2,0,1:T(8,128)(2,1)} %bitcast.175), calls=%async_computation.3 | async-start | bytes 3145728 | tf_op jit(solution)/shard_map/all_to_all | solution.py:122
  326.2 11.9 %convert_bitcast_fusion = bf16[1,1024,4096]{2,1,0:T(8,128)(2,1)} fusion(bf16[768,1024]{0,1:T(8,128)(2,1)} %bitcast.178, bf16[1,768,4096]{2,1,0:T(8,128)(2,1)} %all-gather.10.cloned.1.call-done), kind=kOutput, calls=%fused_computation.25 | convolution fusion | flops 6446645248 | bytes 16252928 | tf_op jit(solution)/shard_map/sk,sd->kd/dot_general | solution.py:65
  338.1 6.7 %fusion.25 = bf16[1,4096,256]{2,1,0:T(8,128)(2,1)} fusion(bf16[768,256]{1,0:T(8,128)(2,1)S(1)} %copy-done.7, f32[4096]{0:T(1024)S(1)} %bitcast.187, f32[768]{0:T(1024)S(1)} %add_rsqrt_fusion, bf16[1,768,4096]{2,1,0:T(8,128)(2,1)} %all-gather.8.cloned.1.call-done), kind=kOutput, calls=%fused_computation.33 | convolution fusion | flops 1624244224 | bytes 8801280 | tf_op jit(solution)/shard_map/sd,sk->dk/dot_general | solution.py:106
  344.7 36.8 %reduce-scatter.4.cloned.1.call-done = bf16[768,1024]{1,0:T(8,128)(2,1)} async-done(((bf16[768,4096]{1,0:T(8,128)(2,1)}), bf16[768,1024]{1,0:T(8,128)(2,1)}) %reduce-scatter.4.cloned.1.call-update) | async-done | bytes 1572880 | tf_op jit(solution)/shard_map/reduce_scatter | solution.py:60
  381.6 3.7 fusion.45
  385.3 10.7 %psum.7 = f32[1,4096]{1,0:T(1,128)} all-reduce(f32[1,4096]{1,0:T(1,128)S(1)} %bitcast.188), channel_id=1, replica_groups=mesh['section'=8,'tp'=4] {'tp'}, use_global_device_ids=true, to_apply=%region_8.9 | all-reduce | flops 4096 | bytes 32768 | tf_op jit(solution)/shard_map/psum | solution.py:118
  396.0 0.0 all-to-all-done
  396.0 2.7 copy.83
  (10 shorter events, 0.0 us)
Async XLA Ops:
  7.2 90.1 %copy-start = (bf16[1,4096,256]{2,1,0:T(8,128)(2,1)S(1)}, bf16[1,4096,256]{2,1,0:T(8,128)(2,1)}, u32[]{:S(2)}) copy-start(bf16[1,4096,256]{2,1,0:T(8,128)(2,1)} %param.9) | copy-start | bytes 6291460
  7.2 90.1 %copy-start.8 = (f32[1,4096]{1,0:T(1,128)S(1)}, f32[1,4096]{1,0:T(1,128)}, u32[]{:S(2)}) copy-start(f32[1,4096]{1,0:T(1,128)} %param.11) | copy-start | bytes 49156
  7.2 85.8 %all-gather.8.cloned.1.call-start = ((), (), s32[]{:S(2)}) async-start(), calls=%async_computation.8 | async-start | bytes 7864320 | tf_op jit(solution)/shard_map/all_gather | solution.py:26
  7.2 40.7 %collective-permute-start = (bf16[1,768,1024]{2,1,0:T(8,128)(2,1)}, bf16[1,768,1024]{2,1,0:T(8,128)(2,1)}, u32[]{:S(2)}, u32[]{:S(2)}) collective-permute-start(bf16[1,768,1024]{2,1,0:T(8,128)(2,1)} %param.6), channel_id=1, source_target_pairs={{0,4},{4,8},{8,12},{12,16},{16,20},{20,24},{24,28},{28,0},{1,5},{5... | collective-permute-start | bytes 4718600 | tf_op jit(solution)/shard_map/ppermute | solution.py:14
  48.0 93.0 %all-gather.10.cloned.1.call-start = ((), (), s32[]{:S(2)}) async-start(), calls=%async_computation.9 | async-start | bytes 7864320 | tf_op jit(solution)/shard_map/all_gather | solution.py:64
  48.1 35.9 %collective-permute-start.1 = (bf16[1,768,1024]{2,1,0:T(8,128)(2,1)}, bf16[1,768,1024]{2,1,0:T(8,128)(2,1)}, u32[]{:S(2)}, u32[]{:S(2)}) collective-permute-start(bf16[1,768,1024]{2,1,0:T(8,128)(2,1)} %param.7), channel_id=1, source_target_pairs={{0,28},{4,0},{8,4},{12,8},{16,12},{20,16},{24,20},{28,24},{1,29},{... | collective-permute-start | bytes 4718600 | tf_op jit(solution)/shard_map/ppermute | solution.py:14
  84.0 87.4 %all-gather.6.cloned.1.call-start = ((), (), s32[]{:S(2)}) async-start(), calls=%async_computation.4 | async-start | bytes 1966080 | tf_op jit(solution)/shard_map/all_gather | solution.py:36
  93.0 4.6 %copy-start.1 = (bf16[1,768,4096]{2,1,0:T(8,128)(2,1)S(1)}, bf16[1,768,4096]{2,1,0:T(8,128)(2,1)}, u32[]{:S(2)}) copy-start(bf16[1,768,4096]{2,1,0:T(8,128)(2,1)} %all-gather.8.cloned.1.call-done) | copy-start | bytes 18874372
  100.3 145.1 %reduce-scatter.6.cloned.1.call-start = ((), (), s32[]{:S(2)}) async-start(), calls=%async_computation.6 | async-start | bytes 1966080 | tf_op jit(solution)/shard_map/reduce_scatter | solution.py:100
  152.0 1.1 copy-start.3
  183.1 7.5 %copy-start.2 = (f32[8,768,128]{1,2,0:T(8,128)S(1)}, f32[8,768,128]{1,2,0:T(8,128)}, u32[]{:S(2)}) copy-start(f32[8,768,128]{1,2,0:T(8,128)} %copy.37) | copy-start | bytes 9437188
  190.6 3.9 copy-start.4
  217.1 96.1 %reduce-scatter.8.cloned.1.call-start = ((), (), s32[]{:S(2)}) async-start(), calls=%async_computation.7 | async-start | bytes 7864320 | tf_op jit(solution)/shard_map/reduce_scatter | solution.py:111
  222.4 1.1 copy-start.5
  254.7 126.9 %reduce-scatter.4.cloned.1.call-start = ((), (), s32[]{:S(2)}) async-start(), calls=%async_computation.5 | async-start | bytes 7864320 | tf_op jit(solution)/shard_map/reduce_scatter | solution.py:60
  266.6 10.3 %copy-start.6 = (bf16[128,8,768]{2,0,1:T(8,128)(2,1)S(1)}, bf16[128,8,768]{2,0,1:T(8,128)(2,1)}, u32[]{:S(2)}) copy-start(bf16[128,8,768]{2,0,1:T(8,128)(2,1)} %copy-done.5) | copy-start | bytes 4718596
  321.6 74.4 %all-to-all-start = ((bf16[192,4,1024]{2,0,1:T(8,128)(2,1)}), bf16[192,4,1024]{2,0,1:T(8,128)(2,1)}, u32[]{:S(2)}, u32[]{:S(2)}) async-start(bf16[192,4,1024]{2,0,1:T(8,128)(2,1)} %bitcast.175), calls=%async_computation.3 | async-start | bytes 3145728 | tf_op jit(solution)/shard_map/all_to_all | solution.py:122
  326.2 11.9 %copy-start.7 = (bf16[768,256]{1,0:T(8,128)(2,1)S(1)}, bf16[768,256]{1,0:T(8,128)(2,1)}, u32[]{:S(2)}) copy-start(bf16[768,256]{1,0:T(8,128)(2,1)} %reduce-scatter.6.cloned.1.call-done) | copy-start | bytes 1179652
Sparse Core Ops, SparseCore 0:
  48.1 44.8 all-gather.7
  94.6 46.3 all-gather.9
  143.1 19.8 all-gather.5
  217.2 28.1 reduce-scatter.5
  254.8 58.3 reduce-scatter.7
  315.6 65.9 reduce-scatter.3
where the time goes:
time: 410 us; the launch traced here: 406 us
  waiting for transfers between devices  190 us (46%)
  matrix products  133 us (32%)
  other arithmetic  35 us (9%)
  between operations  14.5 us (4%)
  local copies, waits for them, and re-layouts  12 us (3%)
  blocking collectives  10.7 us (3%)
  starting transfers between devices  9.8 us (2%)
    ppermute x2, waiting for transfers between devices, shifted(): return lax.ppermute(value, axis, pairs)  71.9 us
    all_gather x1, waiting for transfers between devices, on_device(): dy_all = lax.all_gather(dy_part, 'tp', axis=1, tiled=True)  40.5 us
    reduce_scatter x1, waiting for transfers between devices, on_device(): lax.psum_scatter(out_terms.astype(jnp.bfloat16), 'tp', scatter_dimension=...  36.8 us
    reduce_scatter x1, waiting for transfers between devices, on_device(): lax.psum_scatter((from_query + from_keyval).astype(jnp.bfloat16), 'tp', s...  23.6 us
    dot_general x1, matrix products, on_device(): jnp.einsum('sk,dk->sd', d_queries, wq_dev, preferred_element_type=jnp.flo...  13.2 us
    dot_general x1, matrix products, on_device(): jnp.einsum('sd,sk->dk', normed_all, d_queries, preferred_element_type=jnp...  12.7 us
    dot_general x1, matrix products, on_device(): jnp.dot(normed_all, wq_dev, preferred_element_type=jnp.float32)  12.4 us
    dot_general x1, matrix products, on_device(): jnp.einsum('sk,sd->kd', attn_flat, dy_all, preferred_element_type=jnp.flo...  11.9 us
  transfers between devices with their start and end apart: 9, of which 7 were waited for; matrix products, arithmetic and copies ran while one was open for 30% of the time, Pallas kernels for 0%

commit v1 on v0

--- a/solution.py
+++ b/solution.py
@@ -1,6 +1,8 @@
 import jax
 import jax.numpy as jnp
 from jax import lax
+from jax.experimental import pallas as pl
+from jax.experimental.pallas import tpu as pltpu
 from jax.sharding import PartitionSpec as P
 
 HEAD_SIZE = 128
@@ -14,7 +16,217 @@
     return lax.ppermute(value, axis, pairs)
 
 
+NT = (((1,), (1,)), ((), ()))
+TN = (((0,), (0,)), ((), ()))
+BLOCK_ROWS = 256
+
+
+def dot(left, right, dims):
+    return lax.dot_general(left, right, dims, preferred_element_type=jnp.float32)
+
+
+def attend_kernel(q_ref, k_ref, v_ref, out_ref, probs_ref):
+    rows = q_ref.shape[0]
+    for start in range(0, rows, BLOCK_ROWS):
+        stop = start + BLOCK_ROWS
+        here = slice(start, stop)
+        scores = dot(q_ref[here, :], k_ref[:stop, :], NT) * (HEAD_SIZE ** (-0.5))
+        row_ids = lax.broadcasted_iota(jnp.int32, scores.shape, 0) + start
+        col_ids = lax.broadcasted_iota(jnp.int32, scores.shape, 1)
+        scores = jnp.where(row_ids >= col_ids, scores, jnp.float32(-1e30))
+        top = jnp.max(scores, axis=-1, keepdims=True)
+        powers = jnp.exp(scores - top)
+        probs = powers * (1.0 / jnp.sum(powers, axis=-1, keepdims=True))
+        probs = probs.astype(jnp.bfloat16)
+        probs_ref[0, here, :stop] = probs
+        out_ref[here, :] = jnp.dot(
+            probs, v_ref[:stop, :], preferred_element_type=jnp.float32
+        ).astype(jnp.bfloat16)
+
+
+def attend(queries, keys, values):
+    rows = queries.shape[0]
+    heads = queries.shape[1] // HEAD_SIZE
+    column = pl.BlockSpec((rows, HEAD_SIZE), lambda h: (0, h))
+    fixed = pl.BlockSpec((rows, HEAD_SIZE), lambda h: (0, 0))
+    return pl.pallas_call(
+        attend_kernel,
+        grid=(heads,),
+        in_specs=[column, fixed, fixed],
+        out_specs=[column, pl.BlockSpec((1, rows, rows), lambda h: (h, 0, 0))],
+        out_shape=[
+            jax.ShapeDtypeStruct(queries.shape, jnp.bfloat16),
+            jax.ShapeDtypeStruct((heads, rows, rows), jnp.bfloat16),
+        ],
+        compiler_params=pltpu.CompilerParams(vmem_limit_bytes=40 << 20),
+        cost_estimate=pl.CostEstimate(
+            flops=16 * heads * rows * rows * HEAD_SIZE,
+            bytes_accessed=2 * heads * rows * (rows + 2 * HEAD_SIZE),
+            transcendentals=heads * rows * rows,
+        ),
+    )(queries, keys, values)
+
+
+def backward_kernel(q_ref, k_ref, v_ref, out_ref, dout_ref, probs_ref, dq_ref, dk_ref, dv_ref):
+    rows = q_ref.shape[0]
+
+    @pl.when(pl.program_id(0) == 0)
+    def _():
+        dk_ref[...] = jnp.zeros_like(dk_ref)
+        dv_ref[...] = jnp.zeros_like(dv_ref)
+
+    for start in range(0, rows, BLOCK_ROWS):
+        stop = start + BLOCK_ROWS
+        here = slice(start, stop)
+        d_out = dout_ref[here, :]
+        delta = jnp.sum(
+            d_out.astype(jnp.float32) * out_ref[here, :].astype(jnp.float32), axis=-1, keepdims=True
+        )
+        probs = probs_ref[0, here, :stop]
+        d_probs = dot(d_out, v_ref[:stop, :], NT)
+        d_scores = probs.astype(jnp.float32) * (d_probs - delta) * (HEAD_SIZE ** (-0.5))
+        d_scores = d_scores.astype(jnp.bfloat16)
+        dq_ref[here, :] = jnp.dot(
+            d_scores, k_ref[:stop, :], preferred_element_type=jnp.float32
+        ).astype(jnp.bfloat16)
+        dk_ref[:stop, :] += dot(d_scores, q_ref[here, :], TN)
+        dv_ref[:stop, :] += dot(probs, d_out, TN)
+
+
+def attend_backward(queries, keys, values, attended, d_attended, probs):
+    rows = queries.shape[0]
+    heads = queries.shape[1] // HEAD_SIZE
+    column = pl.BlockSpec((rows, HEAD_SIZE), lambda h: (0, h))
+    fixed = pl.BlockSpec((rows, HEAD_SIZE), lambda h: (0, 0))
+    return pl.pallas_call(
+        backward_kernel,
+        grid=(heads,),
+        in_specs=[column, fixed, fixed, column, column,
+                  pl.BlockSpec((1, rows, rows), lambda h: (h, 0, 0))],
+        out_specs=[column, fixed, fixed],
+        out_shape=[
+            jax.ShapeDtypeStruct(queries.shape, jnp.bfloat16),
+            jax.ShapeDtypeStruct(keys.shape, jnp.float32),
+            jax.ShapeDtypeStruct(keys.shape, jnp.float32),
+        ],
+        compiler_params=pltpu.CompilerParams(vmem_limit_bytes=40 << 20),
+        cost_estimate=pl.CostEstimate(
+            flops=20 * heads * rows * rows * HEAD_SIZE,
+            bytes_accessed=2 * heads * rows * (rows + 4 * HEAD_SIZE),
+            transcendentals=0,
+        ),
+    )(queries, keys, values, attended, d_attended, probs)
+
+
+def scattered(term, width):
+    me = lax.axis_index("tp")
+    count = lax.axis_size("tp")
+    core_pairs = [(i, i ^ 1) for i in range(count)]
+    far_pairs = [(i, i ^ 2) for i in range(count)]
+    core, row = me % 2, me // 2
+    far, near = 1 - row, row
+
+    def block(r, c):
+        return term((2 * r + c) * width)
+
+    far_other = block(far, 1 - core).astype(jnp.bfloat16)
+    far_arrived = lax.ppermute(far_other, "tp", core_pairs)
+    far_mine = block(far, core)
+    far_sum = (far_mine + far_arrived.astype(jnp.float32)).astype(jnp.bfloat16)
+    across = lax.ppermute(far_sum, "tp", far_pairs)
+    near_other = block(near, 1 - core).astype(jnp.bfloat16)
+    near_arrived = lax.ppermute(near_other, "tp", core_pairs)
+    near_mine = block(near, core)
+    return near_mine + near_arrived.astype(jnp.float32), across
+
+
 def on_device(x_handed, cot_handed, w_query, key_value_weight, w_out, norm_gain):
+    wq_dev = w_query[0]
+    wkv_dev = key_value_weight[0]
+    wo_dev = w_out[0]
+    gain_row = norm_gain[0]
+    features = wq_dev.shape[0]
+    me = lax.axis_index("tp")
+    x_part = shifted(x_handed, "section", 1)[0]
+    cot_late, x_part = lax.optimization_barrier((cot_handed, x_part))
+    dy_part = shifted(cot_late, "section", -1)[0]
+    x_all = lax.all_gather(x_part, "tp", axis=1, tiled=True)
+    width = x_part.shape[1]
+    mine = me * width
+    x_float = x_all.astype(jnp.float32)
+    inv_rms = lax.rsqrt(jnp.mean(x_float * x_float, axis=-1, keepdims=True) + 1e-05)
+    normed_all = (x_float * inv_rms * gain_row).astype(jnp.bfloat16)
+    kv_part = jnp.dot(normed_all, wkv_dev, preferred_element_type=jnp.float32).astype(jnp.bfloat16)
+    key_value_pairs = lax.all_gather(kv_part, "tp", axis=1, tiled=True)
+    queries = jnp.dot(normed_all, wq_dev, preferred_element_type=jnp.float32).astype(jnp.bfloat16)
+    keys = lax.dynamic_slice_in_dim(key_value_pairs, me * HEAD_SIZE, HEAD_SIZE, 1)
+    values = lax.dynamic_slice_in_dim(
+        key_value_pairs, (KEY_VALUE_HEADS + me) * HEAD_SIZE, HEAD_SIZE, 1
+    )
+    keys, dy_part = lax.optimization_barrier((keys, dy_part))
+    dy_all = lax.all_gather(dy_part, "tp", axis=1, tiled=True)
+    attended, probs = attend(queries, keys, values)
+
+    def out_term(first):
+        block = lax.dynamic_slice_in_dim(wo_dev, first, width, 1)
+        return jnp.dot(attended, block, preferred_element_type=jnp.float32)
+
+    mixed_near, mixed_far = scattered(out_term, width)
+    layer_out = (
+        x_part.astype(jnp.float32) + mixed_near + mixed_far.astype(jnp.float32)
+    ).astype(jnp.bfloat16)
+    d_attended = dot(dy_all, wo_dev, NT).astype(jnp.bfloat16)
+    d_queries, d_keys, d_values = attend_backward(
+        queries, keys, values, attended, d_attended, probs
+    )
+    pair = jnp.concatenate([d_keys, d_values], axis=1).astype(jnp.bfloat16)
+    pairs = lax.all_gather(pair, "tp", axis=0)
+    d_keyvals = jnp.concatenate(
+        [pairs[g, :, :HEAD_SIZE] for g in range(KEY_VALUE_HEADS)]
+        + [pairs[g, :, HEAD_SIZE:] for g in range(KEY_VALUE_HEADS)],
+        axis=1,
+    )
+    kv_width = wkv_dev.shape[1]
+    d_kv_mine = lax.dynamic_slice_in_dim(d_keyvals, me * kv_width, kv_width, 1)
+    wkv_rows = lax.all_to_all(wkv_dev, "tp", split_axis=0, concat_axis=1, tiled=True)
+
+    def in_term(first):
+        block = lax.dynamic_slice_in_dim(wq_dev, first, width, 0)
+        return dot(d_queries, block, NT)
+
+    d_near, d_far = scattered(in_term, width)
+    grad_out = dot(attended, dy_all, TN).astype(jnp.bfloat16)
+    grad_query = dot(normed_all, d_queries, TN).astype(jnp.bfloat16)
+    grad_keyval = dot(normed_all, d_kv_mine, TN).astype(jnp.bfloat16)
+    from_keyval = dot(d_keyvals, wkv_rows, NT)
+
+    def product(a, b):
+        return jnp.sum(a.astype(jnp.float32) * b.astype(jnp.float32), axis=1)
+
+    sums = jnp.concatenate([
+        product(grad_query, wq_dev) + product(grad_keyval, wkv_dev),
+        product(d_queries, queries) + product(pair, jnp.concatenate([keys, values], axis=1)),
+    ])
+    sums = lax.psum(sums, "tp")
+    grad_gain = sums[:features] / gain_row
+    row_mean = (sums[features:] / features)[:, None]
+    gain_mine = lax.dynamic_slice_in_dim(gain_row, mine, width, 0)
+    unit_mine = x_part.astype(jnp.float32) * inv_rms
+    d_unit = (d_near + from_keyval + d_far.astype(jnp.float32)) * gain_mine
+    grad_in = (
+        dy_part.astype(jnp.float32) + inv_rms * (d_unit - unit_mine * row_mean)
+    ).astype(jnp.bfloat16)
+    return (
+        layer_out[None],
+        grad_in[None],
+        grad_query[None],
+        grad_keyval[None],
+        grad_out[None],
+        grad_gain[None],
+    )
+
+
+def on_device_any(x_handed, cot_handed, w_query, key_value_weight, w_out, norm_gain):
     x_part = shifted(x_handed, "section", 1)[0]
     dy_part = shifted(cot_handed, "section", -1)[0]
     wq_dev = w_query[0]
@@ -132,7 +344,7 @@
 
 def solution(mesh):
     return jax.shard_map(
-        on_device,
+        on_device if mesh.shape["tp"] == KEY_VALUE_HEADS else on_device_any,
         mesh=mesh,
         in_specs=(
             P("section", None, "tp"),

time: 410 us -> 372 us (0.907)
  waiting for transfers between devices: 190 us -> 116 us
  local copies, waits for them, and re-layouts: 12 us -> 53 us
  matrix products: 133 us -> 105 us
  Pallas kernels: 0 us -> 26.3 us
  other arithmetic: 35 us -> 14.3 us
  blocking collectives: 10.7 us -> 22.6 us
  starting transfers between devices: 9.8 us -> 15.5 us
    reduce_scatter x3 -> x0, waiting for transfers between devices: 69.1 us -> none  [the longest x1 36.8 us: on_device(): lax.psum_scatter(out_terms.astype(jnp.bfloat16), 'tp', scatter_dimension=...]
    all_gather x1, waiting for transfers between devices: 40.5 us -> 0.01 us  [on_device(): dy_all = lax.all_gather(dy_part, 'tp', axis=1, tiled=True)]
    unnamed x21 -> x59, local copies, waits for them, and re-layouts: 9.3 us -> 46.3 us
    all_gather x1, waiting for transfers between devices: 8.71 us -> 45 us  [on_device(): x_all = lax.all_gather(x_part, 'tp', axis=1, tiled=True)]
    pallas_call x0 -> x2, Pallas kernels: none -> 26.3 us  [the longest x1 13.3 us: attend_backward(): pl.pallas_call(backward_kernel, grid=(heads,), in_specs=[column, fixed, f...]
    dot_general x12 -> x13, matrix products: 107 us -> 88.5 us  [the longest x9 68.7 us: dot(): lax.dot_general(left, right, dims, preferred_element_type=jnp.float32)]
    ppermute x2, waiting for transfers between devices: 71.9 us -> 55.3 us  [shifted(): return lax.ppermute(value, axis, pairs)]
    all_gather x1, waiting for transfers between devices: 0.01 us -> 15.7 us  [on_device(): key_value_pairs = lax.all_gather(kv_part, 'tp', axis=1, tiled=True)]
  transfers between devices with their start and end apart: 9 -> 13, of which waited for: 7 -> 4; matrix products, arithmetic and copies ran while one was open for 30% -> 41% of each run, Pallas kernels for 0% -> 7%
where the time goes in v1:
time: 372 us; the launch traced here: 367 us
  waiting for transfers between devices  116 us (31%)
  matrix products  105 us (28%)
  local copies, waits for them, and re-layouts  53 us (14%)
  Pallas kernels  26.3 us (7%)
  blocking collectives  22.6 us (6%)
  starting transfers between devices  15.5 us (4%)
  between operations  14.4 us (4%)
  other arithmetic  14.3 us (4%)
    dot_general x9, matrix products, dot(): lax.dot_general(left, right, dims, preferred_element_type=jnp.float32)  68.7 us
    ppermute x2, waiting for transfers between devices, shifted(): return lax.ppermute(value, axis, pairs)  55.3 us
    unnamed x59, local copies, waits for them, and re-layouts  46.3 us
    all_gather x1, waiting for transfers between devices, on_device(): x_all = lax.all_gather(x_part, 'tp', axis=1, tiled=True)  45 us
    psum x1, blocking collectives, on_device(): sums = lax.psum(sums, 'tp')  22.6 us
    dot_general x4, matrix products, out_term(): return jnp.dot(attended, block, preferred_element_type=jnp.float32)  19.8 us
    all_gather x1, waiting for transfers between devices, on_device(): key_value_pairs = lax.all_gather(kv_part, 'tp', axis=1, tiled=True)  15.7 us
    pallas_call x1, Pallas kernels, attend_backward(): pl.pallas_call(backward_kernel, grid=(heads,), in_specs=[column, fixed, f...  13.3 us
  transfers between devices with their start and end apart: 13, of which 4 were waited for; matrix products, arithmetic and copies ran while one was open for 41% of the time, Pallas kernels for 7%

profile of v1, /device:TPU:0, one launch (start us, length us, event | category | flops | bytes accessed | tf_op | source)
XLA Modules:
  0.0 366.8 jit_solution(15564398596246863612)
XLA Ops:
  7.2 0.0 all-gather.5.cloned.1.call-start
  7.2 3.0 collective-permute-start
  10.2 37.6 %collective-permute-done = bf16[1,768,1024]{2,1,0:T(8,128)(2,1)S(1)} collective-permute-done((bf16[1,768,1024]{2,1,0:T(8,128)(2,1)}, bf16[1,768,1024]{2,1,0:T(8,128)(2,1)S(1)}, u32[]{:S(2)}, u32[]{:S(2)}) %collective-permute-start) | collective-permute-done | bytes 1572896 | tf_op jit(solution)/shard_map/ppermute | solution.py:16
  47.8 1.1 copy-done.4
  49.0 0.0 all-gather.7.cloned.1.call-start
  49.1 45.0 %all-gather.5.cloned.1.call-done = bf16[768,4096]{1,0:T(8,128)(2,1)} async-done(((bf16[768,1024]{1,0:T(8,128)(2,1)}), bf16[768,4096]{1,0:T(8,128)(2,1)}) %all-gather.5.cloned.1.call-update) | async-done | bytes 6291472 | tf_op jit(solution)/shard_map/all_gather | solution.py:153
  94.0 4.2 %fusion = f32[768]{0:T(1024)S(1)} fusion(bf16[768,4096]{1,0:T(8,128)(2,1)} %all-gather.5.cloned.1.call-done), kind=kLoop, calls=%fused_computation.3 | loop fusion | flops 9436416 | bytes 6294528 | tf_op jit(solution)/shard_map/reduce_sum | solution.py:157
  98.3 0.3 copy-done.8
  98.6 4.2 %fusion.64 = bf16[768,256]{1,0:T(8,128)(2,1)} fusion(bf16[1,4096,256]{2,1,0:T(8,128)(2,1)} %param.9, bf16[768,4096]{1,0:T(8,128)(2,1)S(1)} %copy-done.8, f32[4096]{0:T(1024)S(1)} %bitcast.128, f32[768]{0:T(1024)S(1)} %add_rsqrt_fusion), kind=kOutput, calls=%fused_computation.60 | convolution fusion | flops 1623392256 | bytes 8801280 | tf_op jit(solution)/shard_map/dot_general | solution.py:159
  102.9 0.0 all-gather.9.cloned.1.call-start
  102.9 4.3 %collective-permute-start.1 = (bf16[1,768,1024]{2,1,0:T(8,128)(2,1)}, bf16[1,768,1024]{2,1,0:T(8,128)(2,1)S(1)}, u32[]{:S(2)}, u32[]{:S(2)}) collective-permute-start(bf16[1,768,1024]{2,1,0:T(8,128)(2,1)} %param.7), channel_id=1, source_target_pairs={{0,28},{4,0},{8,4},{12,8},{16,12},{20,16},{24,20},{28,24},{1,29},{... | collective-permute-start | bytes 4718600 | tf_op jit(solution)/shard_map/ppermute | solution.py:16
  107.2 15.7 %all-gather.7.cloned.1.call-done = bf16[768,1024]{1,0:T(8,128)(2,1)} async-done(((bf16[768,256]{1,0:T(8,128)(2,1)}), bf16[768,1024]{1,0:T(8,128)(2,1)}) %all-gather.7.cloned.1.call-update) | async-done | bytes 1572880 | tf_op jit(solution)/shard_map/all_gather | solution.py:160
  122.9 1.1 constant_dynamic-slice_fusion.1
  123.9 17.7 %collective-permute-done.1 = bf16[1,768,1024]{2,1,0:T(8,128)(2,1)S(1)} collective-permute-done((bf16[1,768,1024]{2,1,0:T(8,128)(2,1)}, bf16[1,768,1024]{2,1,0:T(8,128)(2,1)S(1)}, u32[]{:S(2)}, u32[]{:S(2)}) %collective-permute-start.1) | collective-permute-done | bytes 1572896 | tf_op jit(solution)/shard_map/ppermute | solution.py:16
  141.6 1.2 copy-done.6
  142.8 4.4 %all-to-all-start = ((bf16[4,1024,256]{2,1,0:T(8,128)(2,1)}), bf16[4,1024,256]{2,1,0:T(8,128)(2,1)}, u32[]{:S(2)}, u32[]{:S(2)}) async-start(bf16[4,1024,256]{2,1,0:T(8,128)(2,1)} %bitcast.23), calls=%async_computation | async-start | bytes 4194304 | tf_op jit(solution)/shard_map/all_to_all | solution.py:191
  147.3 0.6 all-gather.11.cloned.1.call-start
  147.9 12.0 %fusion.55.q_ref = bf16[768,1024]{1,0:T(8,128)(2,1)S(1)} fusion(bf16[1,4096,1024]{2,1,0:T(8,128)(2,1)} %param.8, bf16[768,4096]{1,0:T(8,128)(2,1)} %all-gather.5.cloned.1.call-done, f32[4096]{0:T(1024)S(1)} %bitcast.129, f32[768]{0:T(1024)S(1)} %add_rsqrt_fusion), kind=kOutput, calls=%fused_computation.57 | convolution fusion | flops 6455820288 | bytes 16272384 | tf_op jit(solution)/shard_map/dot_general | solution.py:161
  159.8 13.0 %shard_map.109 = (bf16[768,1024]{1,0:T(8,128)(2,1)S(1)}, bf16[8,768,768]{2,1,0:T(8,128)(2,1)S(1)}) custom-call(bf16[768,1024]{1,0:T(8,128)(2,1)S(1)} %fusion.55.q_ref, bf16[768,128]{1,0:T(8,128)(2,1)S(1)} %get-tuple-element.17.k_ref, bf16[768,128]{1,0:T(8,128)(2,1)S(1)} %get-tuple-element.50.v_ref), custom_call_target="tpu_custom_call" | custom-call | flops 9663676416 | bytes 12582912 | tf_op jit(solution)/shard_map/pallas_call | solution.py:52
  172.9 3.6 copy-done.3
  176.4 5.1 %fusion.43 = bf16[768,1024]{1,0:T(8,128)(2,1)} fusion(bf16[768,1024]{1,0:T(8,128)(2,1)S(1)} %get-tuple-element.18.out_ref, bf16[1,1024,4096]{2,1,0:T(8,128)(2,1)} %param.10, s32[]{:T(128)S(6)} %select_n.49), kind=kOutput, calls=%fused_computation.53 | convolution fusion | flops 1611399168 | bytes 5242884 | tf_op jit(solution)/shard_map/dot_general | solution.py:172
  181.5 0.4 collective-permute-start.3
  182.0 4.1 %copy.26 = bf16[1,4096,256]{1,2,0:T(8,128)(2,1)} copy(bf16[1,4096,256]{2,1,0:T(8,128)(2,1)} %param.9) | data formatting | bytes 4194304 | tf_op args[3]
  186.0 11.9 %copy.25 = bf16[1,4096,1024]{1,2,0:T(8,128)(2,1)} copy(bf16[1,4096,1024]{2,1,0:T(8,128)(2,1)} %param.8) | data formatting | bytes 16777216 | tf_op args[2]
  197.9 0.6 constant_dynamic-slice_fusion
  198.5 4.0 %copy.27 = bf16[1024,4,256]{0,2,1:T(8,128)(2,1)} copy(bf16[1024,4,256]{2,0,1:T(8,128)(2,1)} %bitcast.24) | data formatting | bytes 4194304 | tf_op jit(solution)/shard_map/all_to_all | solution.py:191
  202.6 4.6 %fusion.40 = bf16[768,1024]{1,0:T(8,128)(2,1)} fusion(bf16[768,1024]{1,0:T(8,128)(2,1)S(1)} %get-tuple-element.18.out_ref, bf16[1,1024,4096]{2,1,0:T(8,128)(2,1)} %param.10, s32[]{:T(128)S(6)} %select_n.47), kind=kOutput, calls=%fused_computation.52 | convolution fusion | flops 1611399168 | bytes 5242884 | tf_op jit(solution)/shard_map/dot_general | solution.py:172
  207.2 0.1 collective-permute-start.2
  207.2 5.1 %fusion.30 = f32[768,1024]{1,0:T(8,128)} fusion(bf16[768,1024]{1,0:T(8,128)(2,1)S(1)} %get-tuple-element.18.out_ref, bf16[1,1024,4096]{2,1,0:T(8,128)(2,1)} %param.10, s32[]{:T(128)S(6)} %select_n.46), kind=kOutput, calls=%fused_computation.42 | convolution fusion | flops 1610612736 | bytes 6815748 | tf_op jit(solution)/shard_map/dot_general | solution.py:172
  212.4 5.0 %add_convert_fusion.1 = bf16[768,1024]{1,0:T(8,128)(2,1)} fusion(bf16[768,1024]{1,0:T(8,128)(2,1)} %collective-permute-done.3, bf16[768,1024]{1,0:T(8,128)(2,1)S(1)} %get-tuple-element.18.out_ref, bf16[1,1024,4096]{2,1,0:T(8,128)(2,1)} %param.10, s32[]{:T(128)S(6)} %select_n.48), kind=kOutput, calls=%fused_computation.25 | convolution fusion | flops 1612972032 | bytes 6815748 | tf_op jit(solution)/shard_map/dot_general | solution.py:172
  217.4 1.8 collective-permute-start.4
  219.2 11.2 %fusion.52.dout_ref = bf16[768,1024]{1,0:T(8,128)(2,1)S(1)} fusion(bf16[768,4096]{1,0:T(8,128)(2,1)} %all-gather.9.cloned.1.call-done, bf16[1,1024,4096]{2,1,0:T(8,128)(2,1)} %param.10), kind=kOutput, calls=%fused_computation.56 | convolution fusion | flops 6443237376 | bytes 16252928 | tf_op jit(solution)/shard_map/dot_general | solution.py:25
  230.4 13.3 %shard_map.110 = (bf16[768,1024]{1,0:T(8,128)(2,1)S(1)}, f32[768,128]{1,0:T(8,128)S(1)}, f32[768,128]{1,0:T(8,128)S(1)}) custom-call(bf16[768,1024]{1,0:T(8,128)(2,1)S(1)} %fusion.55.q_ref, bf16[768,128]{1,0:T(8,128)(2,1)S(1)} %get-tuple-element.17.k_ref, bf16[768,128]{1,0:T(8,128)(2,1)S(1)} %get-tuple-element.50.v_ref, bf16[768,1024]{1,0:T(8,128)(2,1)S(1)} %copy-done.1, ...), custom_call_target="tpu_custom_call" | custom-call | flops 12079595520 | bytes 15728640 | tf_op jit(solution)/shard_map/pallas_call | solution.py:101
  243.8 0.7 convert.10
  244.5 0.7 convert.11
  245.2 1.1 multiply_reduce_fusion.2
  246.3 4.5 %fusion.49 = bf16[768,1024]{1,0:T(8,128)(2,1)} fusion(bf16[768,1024]{1,0:T(8,128)(2,1)S(1)} %get-tuple-element.21, bf16[1,4096,1024]{2,1,0:T(8,128)(2,1)} %param.8, s32[]{:T(128)S(6)} %select_n.49), kind=kOutput, calls=%fused_computation.55 | convolution fusion | flops 1611399168 | bytes 5242884 | tf_op jit(solution)/shard_map/dot_general | solution.py:25
  250.8 4.6 %fusion.46 = bf16[768,1024]{1,0:T(8,128)(2,1)} fusion(bf16[768,1024]{1,0:T(8,128)(2,1)S(1)} %get-tuple-element.21, bf16[1,4096,1024]{2,1,0:T(8,128)(2,1)} %param.8, s32[]{:T(128)S(6)} %select_n.47), kind=kOutput, calls=%fused_computation.54 | convolution fusion | flops 1611399168 | bytes 5242884 | tf_op jit(solution)/shard_map/dot_general | solution.py:25
  255.4 0.8 pad_maximum_fusion
  256.2 0.1 collective-permute-start.6
  256.3 0.5 collective-permute-start.5
  256.8 15.4 %multiply_reduce_fusion = (f32[4096]{0:T(1024)}, bf16[4096,1024]{0,1:T(8,128)(2,1)}) fusion(bf16[1,4096,1024]{1,2,0:T(8,128)(2,1)} %copy.25, bf16[768,1024]{1,0:T(8,128)(2,1)S(1)} %get-tuple-element.21, bf16[768,4096]{1,0:T(8,128)(2,1)} %all-gather.5.cloned.1.call-done, f32[4096]{0:T(1024)S(1)} %bitcast.130, f32[768]{0:T(1024)S(1)} %copy-done.21), kind=kOutput, calls=%fused_computation | convolution fusion | flops 6476001280 | bytes 24677376 | tf_op jit(solution)/shard_map/dot_general | solution.py:25
  272.2 12.0 %copy.28 = bf16[1,4096,1024]{2,1,0:T(8,128)(2,1)} copy(bf16[1,4096,1024]{1,2,0:T(8,128)(2,1)} %bitcast.121) | data formatting | bytes 16777216
  284.2 0.2 multiply_reduce_fusion.3
  284.4 0.6 add.120
  285.0 5.2 %fusion.22 = f32[768,1024]{1,0:T(8,128)} fusion(bf16[768,1024]{1,0:T(8,128)(2,1)S(1)} %get-tuple-element.21, bf16[1,4096,1024]{2,1,0:T(8,128)(2,1)} %param.8, s32[]{:T(128)S(6)} %select_n.46), kind=kOutput, calls=%fused_computation.34 | convolution fusion | flops 1610612736 | bytes 6815748 | tf_op jit(solution)/shard_map/dot_general | solution.py:25
  290.2 12.0 %convert_bitcast_fusion = bf16[1,1024,4096]{2,1,0:T(8,128)(2,1)} fusion(bf16[768,1024]{1,0:T(8,128)(2,1)S(1)} %copy-done.2, bf16[768,4096]{1,0:T(8,128)(2,1)} %all-gather.9.cloned.1.call-done), kind=kOutput, calls=%fused_computation.10 | convolution fusion | flops 6446645248 | bytes 16252928 | tf_op jit(solution)/shard_map/dot_general | solution.py:25
  302.2 5.0 %add_convert_fusion = bf16[768,1024]{1,0:T(8,128)(2,1)} fusion(bf16[768,1024]{1,0:T(8,128)(2,1)} %collective-permute-done.6, bf16[768,1024]{1,0:T(8,128)(2,1)S(1)} %get-tuple-element.21, bf16[1,4096,1024]{2,1,0:T(8,128)(2,1)} %param.8, s32[]{:T(128)S(6)} %select_n.48), kind=kOutput, calls=%fused_computation.24 | convolution fusion | flops 1612972032 | bytes 6815748 | tf_op jit(solution)/shard_map/dot_general | solution.py:25
  307.3 0.2 collective-permute-start.7
  307.5 1.1 fusion.75
  308.6 1.0 fusion.74
  309.6 1.0 fusion.73
  310.6 1.0 fusion.72
  311.6 1.0 fusion.71
  312.5 1.0 fusion.70
  313.5 1.0 fusion.69
  314.5 1.0 fusion.68
  315.6 7.3 %multiply_reduce_fusion.1 = (f32[4096]{0:T(1024)S(1)}, bf16[4096,256]{0,1:T(8,128)(2,1)}) fusion(bf16[1,4096,256]{1,2,0:T(8,128)(2,1)S(1)} %copy-done.11, bf16[768,1024]{1,0:T(8,128)(2,1)S(1)} %fusion.68, s32[]{:T(128)S(6)} %select_n.51, bf16[768,4096]{1,0:T(8,128)(2,1)} %all-gather.5.cloned.1.call-done, f32[4096]{0:T(1024)S(1)} %bitcast.131, ...), kind=kOutput, calls=%fused_computation.13 | convolution fusion | flops 1628434432 | bytes 10915844 | tf_op jit(solution)/shard_map/dot_general | solution.py:25
  322.9 4.2 %copy.29 = bf16[1,4096,256]{2,1,0:T(8,128)(2,1)} copy(bf16[1,4096,256]{1,2,0:T(8,128)(2,1)} %bitcast.127) | data formatting | bytes 4194304
  327.2 22.6 %psum.7 = f32[4864]{0:T(1024)S(1)} all-reduce(f32[4864]{0:T(1024)S(1)} %pad_maximum_fusion.1), channel_id=1, replica_groups=mesh['section'=8,'tp'=4] {'tp'}, use_global_device_ids=true, to_apply=%region_5.6 | all-reduce | flops 4864 | bytes 38912 | tf_op jit(solution)/shard_map/psum | solution.py:210
  349.8 0.6 slice_divide_fusion
  350.4 3.3 fusion.89
  353.8 0.8 copy-done.10
  354.6 5.4 %fusion.59 = (bf16[1,768,1024]{2,1,0:T(8,128)(2,1)}, bf16[1,768,1024]{2,1,0:T(8,128)(2,1)}) fusion(f32[768]{0:T(1024)S(1)} %slice_multiply_fusion, bf16[768,1024]{1,0:T(8,128)(2,1)S(1)} %bitcast.123, f32[1024]{0:T(1024)S(1)} %bitcast.134, bf16[768,1024]{1,0:T(8,128)(2,1)} %collective-permute-done.7, f32[768,1024]{1,0:T(8,128)S(1)} %fusion.89, ...), kind=kLoop, calls=%fused_computation.59 | loop fusion | flops 15728640 | bytes 22030336 | tf_op jit(solution)/shard_map/broadcast_in_dim | solution.py:221
  (62 shorter events, 0.2 us)
Async XLA Ops:
  7.2 86.8 %all-gather.5.cloned.1.call-start = ((), (), s32[]{:S(2)}) async-start(), calls=%async_computation.1 | async-start | bytes 7864320 | tf_op jit(solution)/shard_map/all_gather | solution.py:153
  7.2 40.6 %collective-permute-start = (bf16[1,768,1024]{2,1,0:T(8,128)(2,1)}, bf16[1,768,1024]{2,1,0:T(8,128)(2,1)S(1)}, u32[]{:S(2)}, u32[]{:S(2)}) collective-permute-start(bf16[1,768,1024]{2,1,0:T(8,128)(2,1)} %param.6), channel_id=1, source_target_pairs={{0,4},{4,8},{8,12},{12,16},{16,20},{20,24},{24,28},{28,0},{1,5},{5... | collective-permute-start | bytes 4718600 | tf_op jit(solution)/shard_map/ppermute | solution.py:16
  47.8 1.1 copy-start.4
  47.8 50.4 %copy-start.15 = (f32[1,4096]{1,0:T(1,128)S(1)}, f32[1,4096]{1,0:T(1,128)}, u32[]{:S(2)}) copy-start(f32[1,4096]{1,0:T(1,128)} %param.11) | copy-start | bytes 49156
  49.0 73.9 %all-gather.7.cloned.1.call-start = ((), (), s32[]{:S(2)}) async-start(), calls=%async_computation.2 | async-start | bytes 1966080 | tf_op jit(solution)/shard_map/all_gather | solution.py:160
  94.0 4.6 %copy-start.8 = (bf16[768,4096]{1,0:T(8,128)(2,1)S(1)}, bf16[768,4096]{1,0:T(8,128)(2,1)}, u32[]{:S(2)}) copy-start(bf16[768,4096]{1,0:T(8,128)(2,1)} %all-gather.5.cloned.1.call-done) | copy-start | bytes 18874372
  98.2 49.6 %copy-start.20 = (f32[768]{0:T(1024)}, f32[768]{0:T(1024)S(1)}, u32[]{:S(2)}) copy-start(f32[768]{0:T(1024)S(1)} %add_rsqrt_fusion) | copy-start | bytes 9220
  102.9 116.3 %all-gather.9.cloned.1.call-start = ((), (), s32[]{:S(2)}) async-start(), calls=%async_computation.3 | async-start | bytes 7864320 | tf_op jit(solution)/shard_map/all_gather | solution.py:167
  102.9 38.7 %collective-permute-start.1 = (bf16[1,768,1024]{2,1,0:T(8,128)(2,1)}, bf16[1,768,1024]{2,1,0:T(8,128)(2,1)S(1)}, u32[]{:S(2)}, u32[]{:S(2)}) collective-permute-start(bf16[1,768,1024]{2,1,0:T(8,128)(2,1)} %param.7), channel_id=1, source_target_pairs={{0,28},{4,0},{8,4},{12,8},{16,12},{20,16},{24,20},{28,24},{1,29},{... | collective-permute-start | bytes 4718600 | tf_op jit(solution)/shard_map/ppermute | solution.py:16
  141.6 1.2 copy-start.6
  142.8 55.7 %all-to-all-start = ((bf16[4,1024,256]{2,1,0:T(8,128)(2,1)}), bf16[4,1024,256]{2,1,0:T(8,128)(2,1)}, u32[]{:S(2)}, u32[]{:S(2)}) async-start(bf16[4,1024,256]{2,1,0:T(8,128)(2,1)} %bitcast.23), calls=%async_computation | async-start | bytes 4194304 | tf_op jit(solution)/shard_map/all_to_all | solution.py:191
  147.3 160.2 %all-gather.11.cloned.1.call-start = ((), (), s32[]{:S(2)}) async-start(), calls=%async_computation.4 | async-start | bytes 1966080 | tf_op jit(solution)/shard_map/all_gather | solution.py:183
  172.9 3.6 copy-start.3
  176.4 35.9 %copy-start = (bf16[768,1024]{1,0:T(8,128)(2,1)}, bf16[768,1024]{1,0:T(8,128)(2,1)S(1)}, u32[]{:S(2)}) copy-start(bf16[768,1024]{1,0:T(8,128)(2,1)S(1)} %get-tuple-element.18.out_ref) | copy-start | bytes 4718596
  181.5 30.8 %collective-permute-start.3 = (bf16[768,1024]{1,0:T(8,128)(2,1)}, bf16[768,1024]{1,0:T(8,128)(2,1)}, u32[]{:S(2)}, u32[]{:S(2)}) collective-permute-start(bf16[768,1024]{1,0:T(8,128)(2,1)} %fusion.43), channel_id=1, source_target_pairs={{0,1},{1,0},{2,3},{3,2},{4,5},{5,4},{6,7},{7,6},{8,9},{9,8},{10,11... | collective-permute-start | bytes 4718600 | tf_op jit(solution)/shard_map/ppermute | solution.py:133
  207.2 146.6 %collective-permute-start.2 = (bf16[768,1024]{1,0:T(8,128)(2,1)}, bf16[768,1024]{1,0:T(8,128)(2,1)}, u32[]{:S(2)}, u32[]{:S(2)}) collective-permute-start(bf16[768,1024]{1,0:T(8,128)(2,1)} %fusion.40), channel_id=1, source_target_pairs={{0,1},{1,0},{2,3},{3,2},{4,5},{5,4},{6,7},{7,6},{8,9},{9,8},{10,11... | collective-permute-start | bytes 4718600 | tf_op jit(solution)/shard_map/ppermute | solution.py:138
  217.4 136.4 %collective-permute-start.4 = (bf16[768,1024]{1,0:T(8,128)(2,1)}, bf16[768,1024]{1,0:T(8,128)(2,1)}, u32[]{:S(2)}, u32[]{:S(2)}) collective-permute-start(bf16[768,1024]{1,0:T(8,128)(2,1)} %add_convert_fusion.1), channel_id=1, source_target_pairs={{0,2},{1,3},{2,0},{3,1},{4,6},{5,7},{6,4},{7,5},{8,10},{9,11},{10,... | collective-permute-start | bytes 4718600 | tf_op jit(solution)/shard_map/ppermute | solution.py:136
  219.2 11.2 %copy-start.1 = (bf16[768,1024]{1,0:T(8,128)(2,1)S(1)}, bf16[768,1024]{1,0:T(8,128)(2,1)}, u32[]{:S(2)}) copy-start(bf16[768,1024]{1,0:T(8,128)(2,1)} %copy-done) | copy-start | bytes 4718596
  250.8 6.0 %copy-start.21 = (f32[768]{0:T(1024)S(1)}, f32[768]{0:T(1024)}, u32[]{:S(2)}) copy-start(f32[768]{0:T(1024)} %copy-done.20) | copy-start | bytes 9220
  256.2 46.0 %collective-permute-start.6 = (bf16[768,1024]{1,0:T(8,128)(2,1)}, bf16[768,1024]{1,0:T(8,128)(2,1)}, u32[]{:S(2)}, u32[]{:S(2)}) collective-permute-start(bf16[768,1024]{1,0:T(8,128)(2,1)} %fusion.49), channel_id=1, source_target_pairs={{0,1},{1,0},{2,3},{3,2},{4,5},{5,4},{6,7},{7,6},{8,9},{9,8},{10,11... | collective-permute-start | bytes 4718600 | tf_op jit(solution)/shard_map/ppermute | solution.py:133
  256.3 97.5 %collective-permute-start.5 = (bf16[768,1024]{1,0:T(8,128)(2,1)}, bf16[768,1024]{1,0:T(8,128)(2,1)}, u32[]{:S(2)}, u32[]{:S(2)}) collective-permute-start(bf16[768,1024]{1,0:T(8,128)(2,1)} %fusion.46), channel_id=1, source_target_pairs={{0,1},{1,0},{2,3},{3,2},{4,5},{5,4},{6,7},{7,6},{8,9},{9,8},{10,11... | collective-permute-start | bytes 4718600 | tf_op jit(solution)/shard_map/ppermute | solution.py:138
  272.2 12.0 %copy-start.13 = (bf16[768,128]{1,0:T(8,128)(2,1)S(1)}, bf16[768,128]{1,0:T(8,128)(2,1)}, u32[]{:S(2)}) copy-start(bf16[768,128]{1,0:T(8,128)(2,1)} %convert.10) | copy-start | bytes 589828
  272.2 12.0 %copy-start.14 = (bf16[768,128]{1,0:T(8,128)(2,1)S(1)}, bf16[768,128]{1,0:T(8,128)(2,1)}, u32[]{:S(2)}) copy-start(bf16[768,128]{1,0:T(8,128)(2,1)} %convert.11) | copy-start | bytes 589828
  272.2 12.2 %copy-start.17 = (f32[768]{0:T(1024)S(1)}, f32[768]{0:T(1024)}, u32[]{:S(2)}) copy-start(f32[768]{0:T(1024)} %multiply_reduce_fusion.2) | copy-start | bytes 9220
  285.0 5.2 %copy-start.2 = (bf16[768,1024]{1,0:T(8,128)(2,1)S(1)}, bf16[768,1024]{1,0:T(8,128)(2,1)}, u32[]{:S(2)}) copy-start(bf16[768,1024]{1,0:T(8,128)(2,1)} %copy-done) | copy-start | bytes 4718596
  307.3 8.3 %copy-start.11 = (bf16[1,4096,256]{1,2,0:T(8,128)(2,1)S(1)}, bf16[1,4096,256]{1,2,0:T(8,128)(2,1)}, u32[]{:S(2)}) copy-start(bf16[1,4096,256]{1,2,0:T(8,128)(2,1)} %copy.26) | copy-start | bytes 6291460
  307.3 8.3 %copy-start.22 = (f32[768]{0:T(1024)S(1)}, f32[768]{0:T(1024)}, u32[]{:S(2)}) copy-start(f32[768]{0:T(1024)} %copy-done.20) | copy-start | bytes 9220
  307.3 46.5 %collective-permute-start.7 = (bf16[768,1024]{1,0:T(8,128)(2,1)}, bf16[768,1024]{1,0:T(8,128)(2,1)}, u32[]{:S(2)}, u32[]{:S(2)}) collective-permute-start(bf16[768,1024]{1,0:T(8,128)(2,1)} %add_convert_fusion), channel_id=1, source_target_pairs={{0,2},{1,3},{2,0},{3,1},{4,6},{5,7},{6,4},{7,5},{8,10},{9,11},{10,... | collective-permute-start | bytes 4718600 | tf_op jit(solution)/shard_map/ppermute | solution.py:136
  315.6 7.3 %copy-start.16 = (bf16[768,1024]{1,0:T(8,128)(2,1)}, bf16[768,1024]{1,0:T(8,128)(2,1)S(1)}, u32[]{:S(2)}) copy-start(bf16[768,1024]{1,0:T(8,128)(2,1)S(1)} %fusion.68) | copy-start | bytes 4718596
  322.9 4.2 %copy-start.18 = (f32[4096]{0:T(1024)S(1)}, f32[4096]{0:T(1024)}, u32[]{:S(2)}) copy-start(f32[4096]{0:T(1024)} %get-tuple-element.52) | copy-start | bytes 49156
  322.9 4.2 %copy-start.19 = (f32[768]{0:T(1024)S(1)}, f32[768]{0:T(1024)}, u32[]{:S(2)}) copy-start(f32[768]{0:T(1024)} %add.120) | copy-start | bytes 9220
  322.9 27.5 %copy-start.12 = (bf16[1024,4,256]{0,2,1:T(8,128)(2,1)S(1)}, bf16[1024,4,256]{0,2,1:T(8,128)(2,1)}, u32[]{:S(2)}) copy-start(bf16[1024,4,256]{0,2,1:T(8,128)(2,1)} %copy.27) | copy-start | bytes 6291460
  350.4 3.4 copy-start.5
  350.4 3.4 copy-start.7
  350.4 3.4 copy-start.9
  350.4 4.2 %copy-start.10 = (f32[768,1024]{1,0:T(8,128)S(1)}, f32[768,1024]{1,0:T(8,128)}, u32[]{:S(2)}) copy-start(f32[768,1024]{1,0:T(8,128)} %fusion.22) | copy-start | bytes 9437188
  350.4 4.2 %copy-start.23 = (f32[1,1024]{1,0:T(1,128)S(1)}, f32[1,1024]{1,0:T(1,128)}, u32[]{:S(2)}) copy-start(f32[1,1024]{1,0:T(1,128)} %constant_dynamic-slice_fusion) | copy-start | bytes 12292
Sparse Core Ops, SparseCore 0:
  49.1 44.8 all-gather.4
  103.0 19.8 all-gather.6
  142.9 65.3 all-gather.8
  256.3 20.7 all-gather.10

commit v2 on v1

--- a/solution.py
+++ b/solution.py
@@ -148,9 +148,9 @@
     features = wq_dev.shape[0]
     me = lax.axis_index("tp")
     x_part = shifted(x_handed, "section", 1)[0]
-    cot_late, x_part = lax.optimization_barrier((cot_handed, x_part))
-    dy_part = shifted(cot_late, "section", -1)[0]
+    dy_part = shifted(cot_handed, "section", -1)[0]
     x_all = lax.all_gather(x_part, "tp", axis=1, tiled=True)
+    x_all, dy_part = lax.optimization_barrier((x_all, dy_part))
     width = x_part.shape[1]
     mine = me * width
     x_float = x_all.astype(jnp.float32)
@@ -180,39 +180,42 @@
         queries, keys, values, attended, d_attended, probs
     )
     pair = jnp.concatenate([d_keys, d_values], axis=1).astype(jnp.bfloat16)
-    pairs = lax.all_gather(pair, "tp", axis=0)
-    d_keyvals = jnp.concatenate(
-        [pairs[g, :, :HEAD_SIZE] for g in range(KEY_VALUE_HEADS)]
-        + [pairs[g, :, HEAD_SIZE:] for g in range(KEY_VALUE_HEADS)],
+    pairs = lax.all_gather(pair, "tp", axis=1, tiled=True)
+    kv_width = wkv_dev.shape[1]
+    half = KEY_VALUE_HEADS // 2
+    first_kv = 2 * HEAD_SIZE * half * (me % 2) + HEAD_SIZE * (me // 2)
+    d_kv_mine = jnp.concatenate(
+        [
+            lax.dynamic_slice_in_dim(pairs, first_kv + 2 * HEAD_SIZE * g, HEAD_SIZE, 1)
+            for g in range(half)
+        ],
         axis=1,
     )
-    kv_width = wkv_dev.shape[1]
-    d_kv_mine = lax.dynamic_slice_in_dim(d_keyvals, me * kv_width, kv_width, 1)
-    wkv_rows = lax.all_to_all(wkv_dev, "tp", split_axis=0, concat_axis=1, tiled=True)
+    grad_query = dot(normed_all, d_queries, TN).astype(jnp.bfloat16)
+    d_kv_mine, d_queries, grad_query = lax.optimization_barrier((d_kv_mine, d_queries, grad_query))
 
     def in_term(first):
         block = lax.dynamic_slice_in_dim(wq_dev, first, width, 0)
-        return dot(d_queries, block, NT)
+        kv_block = lax.dynamic_slice_in_dim(wkv_dev, first, width, 0)
+        return dot(d_queries, block, NT) + dot(d_kv_mine, kv_block, NT)
 
     d_near, d_far = scattered(in_term, width)
     grad_out = dot(attended, dy_all, TN).astype(jnp.bfloat16)
-    grad_query = dot(normed_all, d_queries, TN).astype(jnp.bfloat16)
     grad_keyval = dot(normed_all, d_kv_mine, TN).astype(jnp.bfloat16)
-    from_keyval = dot(d_keyvals, wkv_rows, NT)
 
     def product(a, b):
         return jnp.sum(a.astype(jnp.float32) * b.astype(jnp.float32), axis=1)
 
-    sums = jnp.concatenate([
-        product(grad_query, wq_dev) + product(grad_keyval, wkv_dev),
-        product(d_queries, queries) + product(pair, jnp.concatenate([keys, values], axis=1)),
-    ])
-    sums = lax.psum(sums, "tp")
-    grad_gain = sums[:features] / gain_row
-    row_mean = (sums[features:] / features)[:, None]
+    row_dot = product(d_queries, queries) + product(
+        pair, jnp.concatenate([keys, values], axis=1)
+    )
+    row_dot = jnp.sum(lax.all_gather(row_dot, "tp"), axis=0)
+    row_mean = (row_dot / features)[:, None]
     gain_mine = lax.dynamic_slice_in_dim(gain_row, mine, width, 0)
     unit_mine = x_part.astype(jnp.float32) * inv_rms
-    d_unit = (d_near + from_keyval + d_far.astype(jnp.float32)) * gain_mine
+    d_normed = d_near + d_far.astype(jnp.float32)
+    grad_gain = lax.all_gather(jnp.sum(d_normed * unit_mine, axis=0), "tp", tiled=True)
+    d_unit = d_normed * gain_mine
     grad_in = (
         dy_part.astype(jnp.float32) + inv_rms * (d_unit - unit_mine * row_mean)
     ).astype(jnp.bfloat16)

time: 372 us -> 316 us (0.85)
  local copies, waits for them, and re-layouts: 53 us -> 8.43 us
  waiting for transfers between devices: 116 us -> 141 us
  matrix products: 105 us -> 92.4 us
  blocking collectives: 22.6 us -> 10.3 us
  starting transfers between devices: 15.5 us -> 6.63 us
    unnamed x59 -> x42, local copies, waits for them, and re-layouts: 46.3 us -> 6.31 us
    all_gather x1, waiting for transfers between devices: 45 us -> 9 us  [on_device(): x_all = lax.all_gather(x_part, 'tp', axis=1, tiled=True)]
    ppermute x2, waiting for transfers between devices: 0.01 us -> 27.6 us  [scattered(): across = lax.ppermute(far_sum, 'tp', far_pairs)]
    psum x1 -> x0, blocking collectives: 22.6 us -> none  [on_device(): sums = lax.psum(sums, 'tp')]
    ppermute x2, waiting for transfers between devices: 55.3 us -> 71.9 us  [shifted(): return lax.ppermute(value, axis, pairs)]
    dot_general x9 -> x12, matrix products: 68.7 us -> 58 us  [dot(): lax.dot_general(left, right, dims, preferred_element_type=jnp.float32)]
    all_gather x0 -> x2, blocking collectives: none -> 10.3 us  [the longest x1 5.17 us: on_device(): lax.all_gather(jnp.sum(d_normed * unit_mine, axis=0), 'tp', tiled=True)]
    all_gather x1, waiting for transfers between devices: 0.01 us -> 8.67 us  [on_device(): dy_all = lax.all_gather(dy_part, 'tp', axis=1, tiled=True)]
  transfers between devices with their start and end apart: 13 -> 12, of which waited for: 4 -> 7; matrix products, arithmetic and copies ran while one was open for 41% -> 30% of each run, Pallas kernels for 7% -> 8%
where the time goes in v2:
time: 316 us; the launch traced here: 312 us
  waiting for transfers between devices  141 us (45%)
  matrix products  92.4 us (29%)
  Pallas kernels  26.6 us (8%)
  between operations  14.6 us (5%)
  other arithmetic  12.8 us (4%)
  blocking collectives  10.3 us (3%)
  local copies, waits for them, and re-layouts  8.43 us (3%)
  starting transfers between devices  6.63 us (2%)
    ppermute x2, waiting for transfers between devices, shifted(): return lax.ppermute(value, axis, pairs)  71.9 us
    dot_general x12, matrix products, dot(): lax.dot_general(left, right, dims, preferred_element_type=jnp.float32)  58 us
    ppermute x2, waiting for transfers between devices, scattered(): across = lax.ppermute(far_sum, 'tp', far_pairs)  27.6 us
    dot_general x4, matrix products, out_term(): return jnp.dot(attended, block, preferred_element_type=jnp.float32)  20.7 us
    all_gather x1, waiting for transfers between devices, on_device(): key_value_pairs = lax.all_gather(kv_part, 'tp', axis=1, tiled=True)  19.9 us
    pallas_call x1, Pallas kernels, attend_backward(): pl.pallas_call(backward_kernel, grid=(heads,), in_specs=[column, fixed, f...  13.5 us
    pallas_call x1, Pallas kernels, attend(): pl.pallas_call(attend_kernel, grid=(heads,), in_specs=[column, fixed, fix...  13 us
    dot_general x1, matrix products, on_device(): jnp.dot(normed_all, wq_dev, preferred_element_type=jnp.float32)  11 us
  transfers between devices with their start and end apart: 12, of which 7 were waited for; matrix products, arithmetic and copies ran while one was open for 30% of the time, Pallas kernels for 8%

profile of v2, /device:TPU:0, one launch (start us, length us, event | category | flops | bytes accessed | tf_op | source)
XLA Modules:
  0.0 312.5 jit_solution(4798684386960715554)
XLA Ops:
  7.2 0.0 copy-start
  7.2 0.0 all-gather.14.cloned.1.call-start
  7.2 3.0 collective-permute-start
  10.2 37.7 %collective-permute-done = bf16[1,768,1024]{2,1,0:T(8,128)(2,1)} collective-permute-done((bf16[1,768,1024]{2,1,0:T(8,128)(2,1)}, bf16[1,768,1024]{2,1,0:T(8,128)(2,1)}, u32[]{:S(2)}, u32[]{:S(2)}) %collective-permute-start) | collective-permute-done | bytes 1572896 | tf_op jit(solution)/shard_map/ppermute | solution.py:16
  48.0 0.0 all-gather.14.cloned.1.call-update
  48.0 0.0 all-gather.8.cloned.1.call-start
  48.0 1.8 collective-permute-start.1
  49.8 34.2 %collective-permute-done.1 = bf16[1,768,1024]{2,1,0:T(8,128)(2,1)} collective-permute-done((bf16[1,768,1024]{2,1,0:T(8,128)(2,1)}, bf16[1,768,1024]{2,1,0:T(8,128)(2,1)}, u32[]{:S(2)}, u32[]{:S(2)}) %collective-permute-start.1) | collective-permute-done | bytes 1572896 | tf_op jit(solution)/shard_map/ppermute | solution.py:16
  84.0 9.0 %all-gather.14.cloned.1.call-done = bf16[1,768,4096]{2,1,0:T(8,128)(2,1)} async-done(((bf16[1,768,1024]{2,1,0:T(8,128)(2,1)}), bf16[1,768,4096]{2,1,0:T(8,128)(2,1)}) %all-gather.14.cloned.1.call-update) | async-done | bytes 6291472 | tf_op jit(solution)/shard_map/all_gather | solution.py:152
  93.0 4.2 %fusion = f32[768]{0:T(1024)S(1)} fusion(bf16[768,4096]{1,0:T(8,128)(2,1)} %bitcast.93), kind=kLoop, calls=%fused_computation.2 | loop fusion | flops 9436416 | bytes 6294528 | tf_op jit(solution)/shard_map/reduce_sum | solution.py:157
  97.3 0.3 copy-done.13
  97.6 2.6 fusion.59
  100.2 0.0 all-gather.8.cloned.1.call-update
  100.3 0.0 all-gather.10.cloned.1.call-start
  100.3 19.9 %all-gather.8.cloned.1.call-done = bf16[768,1024]{1,0:T(8,128)(2,1)} async-done(((bf16[768,256]{1,0:T(8,128)(2,1)}), bf16[768,1024]{1,0:T(8,128)(2,1)}) %all-gather.8.cloned.1.call-update) | async-done | bytes 1572880 | tf_op jit(solution)/shard_map/all_gather | solution.py:160
  120.3 1.1 constant_dynamic-slice_fusion.3
  121.3 0.0 all-gather.10.cloned.1.call-update
  121.3 0.2 all-gather.12.cloned.1.call-start
  121.6 11.0 %fusion.49.q_ref = bf16[768,1024]{1,0:T(8,128)(2,1)S(1)} fusion(bf16[1,4096,1024]{2,1,0:T(8,128)(2,1)} %param.8, bf16[768,4096]{1,0:T(8,128)(2,1)} %bitcast.94, f32[4096]{0:T(1024)S(1)} %bitcast.105, f32[768]{0:T(1024)S(1)} %add_rsqrt_fusion), kind=kOutput, calls=%fused_computation.58 | convolution fusion | flops 6455820288 | bytes 16272384 | tf_op jit(solution)/shard_map/dot_general | solution.py:161
  132.7 0.0 copy-start.5
  132.7 13.0 %shard_map.109 = (bf16[768,1024]{1,0:T(8,128)(2,1)S(1)}, bf16[8,768,768]{2,1,0:T(8,128)(2,1)S(1)}) custom-call(bf16[768,1024]{1,0:T(8,128)(2,1)S(1)} %fusion.49.q_ref, bf16[768,128]{1,0:T(8,128)(2,1)S(1)} %get-tuple-element.20.k_ref, bf16[768,128]{1,0:T(8,128)(2,1)S(1)} %get-tuple-element.35.v_ref), custom_call_target="tpu_custom_call" | custom-call | flops 9663676416 | bytes 12582912 | tf_op jit(solution)/shard_map/pallas_call | solution.py:52
  145.7 3.6 %copy-done.12 = bf16[8,768,768]{2,1,0:T(8,128)(2,1)} copy-done((bf16[8,768,768]{2,1,0:T(8,128)(2,1)}, bf16[8,768,768]{2,1,0:T(8,128)(2,1)S(1)}, u32[]{:S(2)}) %copy-start.12) | copy-done | bytes 9437208
  149.4 5.2 %fusion.43 = bf16[768,1024]{1,0:T(8,128)(2,1)} fusion(bf16[768,1024]{1,0:T(8,128)(2,1)S(1)} %get-tuple-element.21.out_ref, bf16[1,1024,4096]{2,1,0:T(8,128)(2,1)} %param.10, s32[]{:T(128)S(6)} %select_n.57), kind=kOutput, calls=%fused_computation.56 | convolution fusion | flops 1611399168 | bytes 5242884 | tf_op jit(solution)/shard_map/dot_general | solution.py:172
  154.5 0.2 collective-permute-start.2
  154.7 4.5 %fusion.46 = bf16[768,1024]{1,0:T(8,128)(2,1)} fusion(bf16[768,1024]{1,0:T(8,128)(2,1)S(1)} %get-tuple-element.21.out_ref, bf16[1,1024,4096]{2,1,0:T(8,128)(2,1)} %param.10, s32[]{:T(128)S(6)} %select_n.59), kind=kOutput, calls=%fused_computation.57 | convolution fusion | flops 1611399168 | bytes 5242884 | tf_op jit(solution)/shard_map/dot_general | solution.py:172
  159.3 0.3 collective-permute-start.3
  159.6 8.7 %all-gather.10.cloned.1.call-done = bf16[768,4096]{1,0:T(8,128)(2,1)} async-done(((bf16[768,1024]{1,0:T(8,128)(2,1)}), bf16[768,4096]{1,0:T(8,128)(2,1)}) %all-gather.10.cloned.1.call-update) | async-done | bytes 6291472 | tf_op jit(solution)/shard_map/all_gather | solution.py:167
  168.3 11.1 %fusion.52.dout_ref = bf16[768,1024]{1,0:T(8,128)(2,1)S(1)} fusion(bf16[768,4096]{1,0:T(8,128)(2,1)} %all-gather.10.cloned.1.call-done, bf16[1,1024,4096]{2,1,0:T(8,128)(2,1)} %param.10), kind=kOutput, calls=%fused_computation.59 | convolution fusion | flops 6443237376 | bytes 16252928 | tf_op jit(solution)/shard_map/dot_general | solution.py:25
  179.4 13.5 %shard_map.110 = (bf16[768,1024]{1,0:T(8,128)(2,1)S(1)}, f32[768,128]{1,0:T(8,128)S(1)}, f32[768,128]{1,0:T(8,128)S(1)}) custom-call(bf16[768,1024]{1,0:T(8,128)(2,1)S(1)} %copy-done.6, bf16[768,128]{1,0:T(8,128)(2,1)S(1)} %get-tuple-element.20.k_ref, bf16[768,128]{1,0:T(8,128)(2,1)S(1)} %get-tuple-element.35.v_ref, bf16[768,1024]{1,0:T(8,128)(2,1)S(1)} %copy-done.9, ...), custom_call_target="tpu_custom_call" | custom-call | flops 12079595520 | bytes 15728640 | tf_op jit(solution)/shard_map/pallas_call | solution.py:101
  192.9 0.0 copy-start.1
  192.9 1.1 copy-done.1
  194.1 0.9 pad_maximum_fusion
  195.0 0.0 all-gather.12.cloned.1.call-update
  195.0 0.0 copy-start.10
  195.0 5.6 %fusion.31 = f32[768,1024]{1,0:T(8,128)} fusion(bf16[768,1024]{1,0:T(8,128)(2,1)} %copy-done.8, bf16[1,1024,4096]{2,1,0:T(8,128)(2,1)} %param.10, s32[]{:T(128)S(6)} %select_n.56), kind=kOutput, calls=%fused_computation.44 | convolution fusion | flops 1610612736 | bytes 6815748 | tf_op jit(solution)/shard_map/dot_general | solution.py:172
  200.7 0.0 collective-permute-done.3
  200.7 5.4 %add_convert_fusion.3 = bf16[768,1024]{1,0:T(8,128)(2,1)} fusion(bf16[768,1024]{1,0:T(8,128)(2,1)} %collective-permute-done.3, bf16[768,1024]{1,0:T(8,128)(2,1)S(1)} %copy-done.10, bf16[1,1024,4096]{2,1,0:T(8,128)(2,1)} %param.10, s32[]{:T(128)S(6)} %select_n.58), kind=kOutput, calls=%fused_computation.29 | convolution fusion | flops 1612972032 | bytes 6815748 | tf_op jit(solution)/shard_map/dot_general | solution.py:172
  206.1 0.2 collective-permute-start.4
  206.3 9.4 %convolution_convert_fusion = bf16[4096,1024]{1,0:T(8,128)(2,1)} fusion(bf16[768,1024]{1,0:T(8,128)(2,1)S(1)} %copy-done.2, bf16[768,4096]{1,0:T(8,128)(2,1)S(1)} %bitcast.98, f32[4096]{0:T(1024)S(1)} %bitcast.106, f32[768]{0:T(1024)S(1)} %add_rsqrt_fusion), kind=kOutput, calls=%fused_computation.10 | convolution fusion | flops 6459228160 | bytes 16272384 | tf_op jit(solution)/shard_map/dot_general | solution.py:25
  215.7 3.5 %all-gather.12.cloned.1.call-done = bf16[768,1024]{1,0:T(8,128)(2,1)} async-done(((bf16[768,256]{1,0:T(8,128)(2,1)}), bf16[768,1024]{1,0:T(8,128)(2,1)}) %all-gather.12.cloned.1.call-update) | async-done | bytes 1572880 | tf_op jit(solution)/shard_map/all_gather | solution.py:183
  219.2 1.1 constant_dynamic-slice_fusion.2
  220.3 3.9 %fusion.17 = f32[768,1024]{1,0:T(8,128)S(1)} fusion(bf16[768,1024]{1,0:T(8,128)(2,1)} %copy-done.1, bf16[1,4096,1024]{2,1,0:T(8,128)(2,1)} %param.8, s32[]{:T(128)S(6)} %select_n.59), kind=kOutput, calls=%fused_computation.30 | convolution fusion | flops 1610612736 | bytes 6815748 | tf_op jit(solution)/shard_map/dot_general | solution.py:25
  224.2 0.0 copy-start.11
  224.2 1.9 add_convert_fusion.1
  226.1 0.3 collective-permute-start.6
  226.4 12.2 %convert_bitcast_fusion = bf16[1,1024,4096]{2,1,0:T(8,128)(2,1)} fusion(bf16[768,1024]{1,0:T(8,128)(2,1)S(1)} %copy-done.11, bf16[768,4096]{1,0:T(8,128)(2,1)} %all-gather.10.cloned.1.call-done), kind=kOutput, calls=%fused_computation.9 | convolution fusion | flops 6446645248 | bytes 16252928 | tf_op jit(solution)/shard_map/dot_general | solution.py:25
  238.6 0.2 multiply_reduce_fusion.1
  238.8 0.5 multiply_reduce_fusion
  239.3 3.5 %fusion.21 = f32[768,1024]{1,0:T(8,128)S(1)} fusion(bf16[768,1024]{1,0:T(8,128)(2,1)S(1)} %copy-done.3, bf16[1,4096,1024]{2,1,0:T(8,128)(2,1)} %param.8, s32[]{:T(128)S(6)} %select_n.57), kind=kOutput, calls=%fused_computation.34 | convolution fusion | flops 1610612736 | bytes 6815748 | tf_op jit(solution)/shard_map/dot_general | solution.py:25
  242.8 1.8 add_convert_fusion.2
  244.6 0.3 collective-permute-start.5
  244.8 5.1 %all-gather.2 = f32[4,1,768]{2,1,0:T(1,128)S(1)} all-gather(f32[1,1,768]{2,1,0:T(1,128)S(1)} %reshape.52), channel_id=3, replica_groups=mesh['section'=8,'tp'=4] {'tp'}, dimensions={0}, use_global_device_ids=true | all-gather | bytes 15360 | tf_op jit(solution)/shard_map/all_gather | solution.py:212
  250.0 3.9 %fusion.19 = f32[768,1024]{1,0:T(8,128)S(1)} fusion(bf16[768,1024]{1,0:T(8,128)(2,1)} %copy-done.1, bf16[1,4096,1024]{2,1,0:T(8,128)(2,1)} %param.8, s32[]{:T(128)S(6)} %select_n.58), kind=kOutput, calls=%fused_computation.32 | convolution fusion | flops 1610612736 | bytes 6815748 | tf_op jit(solution)/shard_map/dot_general | solution.py:25
  253.9 2.2 add_convert_fusion
  256.1 0.0 copy-start.4
  256.2 0.3 collective-permute-start.7
  256.4 0.6 fusion.65
  257.1 0.5 copy-done.4
  257.6 3.4 %fusion.23 = f32[768,1024]{1,0:T(8,128)S(1)} fusion(bf16[768,1024]{1,0:T(8,128)(2,1)S(1)} %copy-done.4, bf16[1,4096,1024]{2,1,0:T(8,128)(2,1)} %param.8, s32[]{:T(128)S(6)} %select_n.56), kind=kOutput, calls=%fused_computation.36 | convolution fusion | flops 1610612736 | bytes 6815748 | tf_op jit(solution)/shard_map/dot_general | solution.py:25
  261.0 4.2 %fusion.7 = bf16[1,4096,256]{2,1,0:T(8,128)(2,1)} fusion(bf16[768,256]{1,0:T(8,128)(2,1)S(1)} %pad_maximum_fusion.1, bf16[768,4096]{1,0:T(8,128)(2,1)S(1)} %bitcast.101, f32[4096]{0:T(1024)S(1)} %bitcast.107, f32[768]{0:T(1024)S(1)} %add_rsqrt_fusion), kind=kOutput, calls=%fused_computation.12 | convolution fusion | flops 1624244224 | bytes 8801280 | tf_op jit(solution)/shard_map/dot_general | solution.py:25
  265.2 27.6 %collective-permute-done.7 = bf16[768,1024]{1,0:T(8,128)(2,1)S(1)} collective-permute-done((bf16[768,1024]{1,0:T(8,128)(2,1)S(1)}, bf16[768,1024]{1,0:T(8,128)(2,1)S(1)}, u32[]{:S(2)}, u32[]{:S(2)}) %collective-permute-start.7) | collective-permute-done | bytes 1572896 | tf_op jit(solution)/shard_map/ppermute | solution.py:136
  292.8 6.9 %fusion.14 = (f32[1024]{0:T(1024)S(1)}, bf16[1,768,1024]{2,1,0:T(8,128)(2,1)}, bf16[1,768,1024]{2,1,0:T(8,128)(2,1)}) fusion(bf16[1,768,1024]{2,1,0:T(8,128)(2,1)} %collective-permute-done, f32[768]{0:T(1024)S(1)} %add_rsqrt_fusion, bf16[768,1024]{1,0:T(8,128)(2,1)S(1)} %collective-permute-done.7, bf16[768,1024]{1,0:T(8,128)(2,1)} %collective-permute-done.5, ...), kind=kLoop, calls=%fused_computation.21 | loop fusion | flops 17300480 | bytes 22034432 | tf_op jit(solution)/shard_map/reduce_sum | solution.py:217
  299.7 5.2 %all_gather.24 = f32[4096]{0:T(1024)S(1)} all-gather(f32[1024]{0:T(1024)S(1)} %get-tuple-element.30), channel_id=1, replica_groups=mesh['section'=8,'tp'=4] {'tp'}, dimensions={0}, use_global_device_ids=true | all-gather | bytes 20480 | tf_op jit(solution)/shard_map/all_gather | solution.py:217
  304.9 0.6 copy.13
  (45 shorter events, 0.2 us)
Async XLA Ops:
  7.2 90.1 %copy-start = (bf16[1,4096,256]{2,1,0:T(8,128)(2,1)S(1)}, bf16[1,4096,256]{2,1,0:T(8,128)(2,1)}, u32[]{:S(2)}) copy-start(bf16[1,4096,256]{2,1,0:T(8,128)(2,1)} %param.9) | copy-start | bytes 6291460
  7.2 85.8 %all-gather.14.cloned.1.call-start = ((), (), s32[]{:S(2)}) async-start(), calls=%async_computation.3 | async-start | bytes 7864320 | tf_op jit(solution)/shard_map/all_gather | solution.py:152
  7.2 40.7 %collective-permute-start = (bf16[1,768,1024]{2,1,0:T(8,128)(2,1)}, bf16[1,768,1024]{2,1,0:T(8,128)(2,1)}, u32[]{:S(2)}, u32[]{:S(2)}) collective-permute-start(bf16[1,768,1024]{2,1,0:T(8,128)(2,1)} %param.6), channel_id=1, source_target_pairs={{0,4},{4,8},{8,12},{12,16},{16,20},{20,24},{24,28},{28,0},{1,5},{5... | collective-permute-start | bytes 4718600 | tf_op jit(solution)/shard_map/ppermute | solution.py:16
  48.0 49.3 %copy-start.15 = (f32[1,4096]{1,0:T(1,128)S(1)}, f32[1,4096]{1,0:T(1,128)}, u32[]{:S(2)}) copy-start(f32[1,4096]{1,0:T(1,128)} %param.11) | copy-start | bytes 49156
  48.0 72.3 %all-gather.8.cloned.1.call-start = ((), (), s32[]{:S(2)}) async-start(), calls=%async_computation | async-start | bytes 1966080 | tf_op jit(solution)/shard_map/all_gather | solution.py:160
  48.0 35.9 %collective-permute-start.1 = (bf16[1,768,1024]{2,1,0:T(8,128)(2,1)}, bf16[1,768,1024]{2,1,0:T(8,128)(2,1)}, u32[]{:S(2)}, u32[]{:S(2)}) collective-permute-start(bf16[1,768,1024]{2,1,0:T(8,128)(2,1)} %param.7), channel_id=1, source_target_pairs={{0,28},{4,0},{8,4},{12,8},{16,12},{20,16},{24,20},{28,24},{1,29},{... | collective-permute-start | bytes 4718600 | tf_op jit(solution)/shard_map/ppermute | solution.py:16
  93.0 4.6 %copy-start.13 = (bf16[1,768,4096]{2,1,0:T(8,128)(2,1)S(1)}, bf16[1,768,4096]{2,1,0:T(8,128)(2,1)}, u32[]{:S(2)}) copy-start(bf16[1,768,4096]{2,1,0:T(8,128)(2,1)} %all-gather.14.cloned.1.call-done) | copy-start | bytes 18874372
  100.3 68.0 %all-gather.10.cloned.1.call-start = ((), (), s32[]{:S(2)}) async-start(), calls=%async_computation.1 | async-start | bytes 7864320 | tf_op jit(solution)/shard_map/all_gather | solution.py:167
  121.3 97.9 %all-gather.12.cloned.1.call-start = ((), (), s32[]{:S(2)}) async-start(), calls=%async_computation.2 | async-start | bytes 1966080 | tf_op jit(solution)/shard_map/all_gather | solution.py:183
  132.7 13.0 %copy-start.5 = (bf16[768,1024]{1,0:T(8,128)(2,1)}, bf16[768,1024]{1,0:T(8,128)(2,1)S(1)}, u32[]{:S(2)}) copy-start(bf16[768,1024]{1,0:T(8,128)(2,1)S(1)} %fusion.49.q_ref) | copy-start | bytes 4718596
  145.7 3.7 %copy-start.12 = (bf16[8,768,768]{2,1,0:T(8,128)(2,1)}, bf16[8,768,768]{2,1,0:T(8,128)(2,1)S(1)}, u32[]{:S(2)}) copy-start(bf16[8,768,768]{2,1,0:T(8,128)(2,1)S(1)} %get-tuple-element.23.probs_ref) | copy-start | bytes 28311556
  149.4 5.4 %copy-start.8 = (bf16[768,1024]{1,0:T(8,128)(2,1)}, bf16[768,1024]{1,0:T(8,128)(2,1)S(1)}, u32[]{:S(2)}) copy-start(bf16[768,1024]{1,0:T(8,128)(2,1)S(1)} %get-tuple-element.21.out_ref) | copy-start | bytes 4718596
  154.5 110.7 %collective-permute-start.2 = (bf16[768,1024]{1,0:T(8,128)(2,1)}, bf16[768,1024]{1,0:T(8,128)(2,1)}, u32[]{:S(2)}, u32[]{:S(2)}) collective-permute-start(bf16[768,1024]{1,0:T(8,128)(2,1)} %fusion.43), channel_id=1, source_target_pairs={{0,1},{1,0},{2,3},{3,2},{4,5},{5,4},{6,7},{7,6},{8,9},{9,8},{10,11... | collective-permute-start | bytes 4718600 | tf_op jit(solution)/shard_map/ppermute | solution.py:138
  159.3 41.4 %collective-permute-start.3 = (bf16[768,1024]{1,0:T(8,128)(2,1)}, bf16[768,1024]{1,0:T(8,128)(2,1)}, u32[]{:S(2)}, u32[]{:S(2)}) collective-permute-start(bf16[768,1024]{1,0:T(8,128)(2,1)} %fusion.46), channel_id=1, source_target_pairs={{0,1},{1,0},{2,3},{3,2},{4,5},{5,4},{6,7},{7,6},{8,9},{9,8},{10,11... | collective-permute-start | bytes 4718600 | tf_op jit(solution)/shard_map/ppermute | solution.py:133
  168.3 11.1 %copy-start.6 = (bf16[768,1024]{1,0:T(8,128)(2,1)S(1)}, bf16[768,1024]{1,0:T(8,128)(2,1)}, u32[]{:S(2)}) copy-start(bf16[768,1024]{1,0:T(8,128)(2,1)} %copy-done.5) | copy-start | bytes 4718596
  168.3 11.1 %copy-start.9 = (bf16[768,1024]{1,0:T(8,128)(2,1)S(1)}, bf16[768,1024]{1,0:T(8,128)(2,1)}, u32[]{:S(2)}) copy-start(bf16[768,1024]{1,0:T(8,128)(2,1)} %copy-done.8) | copy-start | bytes 4718596
  192.9 1.1 copy-start.1
  195.0 5.7 %copy-start.10 = (bf16[768,1024]{1,0:T(8,128)(2,1)S(1)}, bf16[768,1024]{1,0:T(8,128)(2,1)}, u32[]{:S(2)}) copy-start(bf16[768,1024]{1,0:T(8,128)(2,1)} %copy-done.8) | copy-start | bytes 4718596
  195.0 11.3 %slice-start = ((s8[6291456]{0:T(1024)(128)(4,1)}), s8[4194304]{0:T(1024)(128)(4,1)S(1)}, s32[]{:S(2)}) async-start(s8[6291456]{0:T(1024)(128)(4,1)} %bitcast.96), calls=%async_computation.4 | async-start | bytes 8388608
  200.7 5.6 %copy-start.2 = (bf16[768,1024]{1,0:T(8,128)(2,1)S(1)}, bf16[768,1024]{1,0:T(8,128)(2,1)}, u32[]{:S(2)}) copy-start(bf16[768,1024]{1,0:T(8,128)(2,1)} %copy-done.1) | copy-start | bytes 4718596
  200.7 5.6 %slice-start.1 = ((s8[6291456]{0:T(1024)(128)(4,1)}), s8[2097152]{0:T(1024)(128)(4,1)S(1)}, s32[]{:S(2)}) async-start(s8[6291456]{0:T(1024)(128)(4,1)} %bitcast.96), calls=%async_computation.5 | async-start | bytes 4194304
  206.1 59.1 %collective-permute-start.4 = (bf16[768,1024]{1,0:T(8,128)(2,1)}, bf16[768,1024]{1,0:T(8,128)(2,1)}, u32[]{:S(2)}, u32[]{:S(2)}) collective-permute-start(bf16[768,1024]{1,0:T(8,128)(2,1)} %add_convert_fusion.3), channel_id=1, source_target_pairs={{0,2},{1,3},{2,0},{3,1},{4,6},{5,7},{6,4},{7,5},{8,10},{9,11},{10,... | collective-permute-start | bytes 4718600 | tf_op jit(solution)/shard_map/ppermute | solution.py:136
  224.2 2.2 copy-start.11
  226.1 12.6 %copy-start.3 = (bf16[768,1024]{1,0:T(8,128)(2,1)S(1)}, bf16[768,1024]{1,0:T(8,128)(2,1)}, u32[]{:S(2)}) copy-start(bf16[768,1024]{1,0:T(8,128)(2,1)} %copy-done.1) | copy-start | bytes 4718596
  226.1 12.7 %copy-start.7 = (bf16[768,1024]{1,0:T(8,128)(2,1)S(1)}, bf16[768,1024]{1,0:T(8,128)(2,1)}, u32[]{:S(2)}) copy-start(bf16[768,1024]{1,0:T(8,128)(2,1)} %copy-done.5) | copy-start | bytes 4718596
  226.1 27.8 %collective-permute-start.6 = (bf16[768,1024]{1,0:T(8,128)(2,1)}, bf16[768,1024]{1,0:T(8,128)(2,1)}, u32[]{:S(2)}, u32[]{:S(2)}) collective-permute-start(bf16[768,1024]{1,0:T(8,128)(2,1)} %add_convert_fusion.1), channel_id=1, source_target_pairs={{0,1},{1,0},{2,3},{3,2},{4,5},{5,4},{6,7},{7,6},{8,9},{9,8},{10,11... | collective-permute-start | bytes 4718600 | tf_op jit(solution)/shard_map/ppermute | solution.py:133
  244.6 20.7 %collective-permute-start.5 = (bf16[768,1024]{1,0:T(8,128)(2,1)}, bf16[768,1024]{1,0:T(8,128)(2,1)}, u32[]{:S(2)}, u32[]{:S(2)}) collective-permute-start(bf16[768,1024]{1,0:T(8,128)(2,1)} %add_convert_fusion.2), channel_id=1, source_target_pairs={{0,1},{1,0},{2,3},{3,2},{4,5},{5,4},{6,7},{7,6},{8,9},{9,8},{10,11... | collective-permute-start | bytes 4718600 | tf_op jit(solution)/shard_map/ppermute | solution.py:138
  253.9 7.1 %slice-start.2 = ((s8[6291456]{0:T(1024)(128)(4,1)}), s8[4194304]{0:T(1024)(128)(4,1)S(1)}, s32[]{:S(2)}) async-start(s8[6291456]{0:T(1024)(128)(4,1)} %bitcast.99), calls=%async_computation.6 | async-start | bytes 8388608
  256.1 1.4 copy-start.4
  256.2 36.7 %collective-permute-start.7 = (bf16[768,1024]{1,0:T(8,128)(2,1)S(1)}, bf16[768,1024]{1,0:T(8,128)(2,1)S(1)}, u32[]{:S(2)}, u32[]{:S(2)}) collective-permute-start(bf16[768,1024]{1,0:T(8,128)(2,1)S(1)} %add_convert_fusion), channel_id=1, source_target_pairs={{0,2},{1,3},{2,0},{3,1},{4,6},{5,7},{6,4},{7,5},{8,10},{9,11},{10,... | collective-permute-start | bytes 4718600 | tf_op jit(solution)/shard_map/ppermute | solution.py:136
  256.4 4.5 %slice-start.3 = ((s8[6291456]{0:T(1024)(128)(4,1)}), s8[2097152]{0:T(1024)(128)(4,1)S(1)}, s32[]{:S(2)}) async-start(s8[6291456]{0:T(1024)(128)(4,1)} %bitcast.99), calls=%async_computation.7 | async-start | bytes 4194304
  261.0 31.8 %copy-start.14 = (f32[768,1024]{1,0:T(8,128)S(1)}, f32[768,1024]{1,0:T(8,128)}, u32[]{:S(2)}) copy-start(f32[768,1024]{1,0:T(8,128)} %fusion.31) | copy-start | bytes 9437188
Sparse Core Ops, SparseCore 0:
  48.1 44.8 all-gather.13
  100.4 19.8 all-gather.7
  121.8 46.3 all-gather.9
  195.1 24.0 all-gather.11

commit v3 on v2

--- a/solution.py
+++ b/solution.py
@@ -118,7 +118,7 @@
     )(queries, keys, values, attended, d_attended, probs)
 
 
-def scattered(term, width):
+def scattered(term, width, operands):
     me = lax.axis_index("tp")
     count = lax.axis_size("tp")
     core_pairs = [(i, i ^ 1) for i in range(count)]
@@ -127,17 +127,18 @@
     far, near = 1 - row, row
 
     def block(r, c):
-        return term((2 * r + c) * width)
+        return term((2 * r + c) * width, *operands)
 
     far_other = block(far, 1 - core).astype(jnp.bfloat16)
     far_arrived = lax.ppermute(far_other, "tp", core_pairs)
     far_mine = block(far, core)
     far_sum = (far_mine + far_arrived.astype(jnp.float32)).astype(jnp.bfloat16)
+    far_sum, operands = lax.optimization_barrier((far_sum, operands))
     across = lax.ppermute(far_sum, "tp", far_pairs)
     near_other = block(near, 1 - core).astype(jnp.bfloat16)
     near_arrived = lax.ppermute(near_other, "tp", core_pairs)
     near_mine = block(near, core)
-    return near_mine + near_arrived.astype(jnp.float32), across
+    return near_mine + near_arrived.astype(jnp.float32), across, operands
 
 
 def on_device(x_handed, cot_handed, w_query, key_value_weight, w_out, norm_gain):
@@ -157,21 +158,25 @@
     inv_rms = lax.rsqrt(jnp.mean(x_float * x_float, axis=-1, keepdims=True) + 1e-05)
     normed_all = (x_float * inv_rms * gain_row).astype(jnp.bfloat16)
     kv_part = jnp.dot(normed_all, wkv_dev, preferred_element_type=jnp.float32).astype(jnp.bfloat16)
-    key_value_pairs = lax.all_gather(kv_part, "tp", axis=1, tiled=True)
+    low, high = kv_part[:, :HEAD_SIZE], kv_part[:, HEAD_SIZE:]
+    edge = (me == 0) | (me == KEY_VALUE_HEADS - 1)
+    first_in = lax.ppermute(
+        jnp.where(edge, high, low), "tp", [(0, 1), (1, 2), (2, 0), (3, 3)]
+    )
+    second_in = lax.ppermute(
+        jnp.where(edge, low, high), "tp", [(0, 0), (1, 3), (2, 1), (3, 2)]
+    )
     queries = jnp.dot(normed_all, wq_dev, preferred_element_type=jnp.float32).astype(jnp.bfloat16)
-    keys = lax.dynamic_slice_in_dim(key_value_pairs, me * HEAD_SIZE, HEAD_SIZE, 1)
-    values = lax.dynamic_slice_in_dim(
-        key_value_pairs, (KEY_VALUE_HEADS + me) * HEAD_SIZE, HEAD_SIZE, 1
-    )
-    keys, dy_part = lax.optimization_barrier((keys, dy_part))
+    keys = jnp.where(edge, second_in, first_in)
+    values = jnp.where(edge, first_in, second_in)
     dy_all = lax.all_gather(dy_part, "tp", axis=1, tiled=True)
     attended, probs = attend(queries, keys, values)
 
-    def out_term(first):
+    def out_term(first, attended):
         block = lax.dynamic_slice_in_dim(wo_dev, first, width, 1)
         return jnp.dot(attended, block, preferred_element_type=jnp.float32)
 
-    mixed_near, mixed_far = scattered(out_term, width)
+    mixed_near, mixed_far, (attended,) = scattered(out_term, width, (attended,))
     layer_out = (
         x_part.astype(jnp.float32) + mixed_near + mixed_far.astype(jnp.float32)
     ).astype(jnp.bfloat16)
@@ -194,12 +199,14 @@
     grad_query = dot(normed_all, d_queries, TN).astype(jnp.bfloat16)
     d_kv_mine, d_queries, grad_query = lax.optimization_barrier((d_kv_mine, d_queries, grad_query))
 
-    def in_term(first):
+    def in_term(first, d_queries, d_kv_mine, *later):
         block = lax.dynamic_slice_in_dim(wq_dev, first, width, 0)
         kv_block = lax.dynamic_slice_in_dim(wkv_dev, first, width, 0)
         return dot(d_queries, block, NT) + dot(d_kv_mine, kv_block, NT)
 
-    d_near, d_far = scattered(in_term, width)
+    d_near, d_far, (d_queries, d_kv_mine, attended, normed_all) = scattered(
+        in_term, width, (d_queries, d_kv_mine, attended, normed_all)
+    )
     grad_out = dot(attended, dy_all, TN).astype(jnp.bfloat16)
     grad_keyval = dot(normed_all, d_kv_mine, TN).astype(jnp.bfloat16)
 

time: 316 us -> 314 us (level)
  waiting for transfers between devices: 141 us -> 124 us
  blocking collectives: 10.3 us -> 22.3 us
  starting transfers between devices: 6.63 us -> 10.7 us
  matrix products: 92.4 us -> 89.2 us
    all_gather x1 -> x0, waiting for transfers between devices: 19.9 us -> none  [on_device(): key_value_pairs = lax.all_gather(kv_part, 'tp', axis=1, tiled=True)]
    all_gather x1, blocking collectives: 5.15 us -> 17.1 us  [on_device(): row_dot = jnp.sum(lax.all_gather(row_dot, 'tp'), axis=0)]
    all_gather x1, waiting for transfers between devices: 8.67 us -> 0.01 us  [on_device(): dy_all = lax.all_gather(dy_part, 'tp', axis=1, tiled=True)]
    all_gather x1, waiting for transfers between devices: 3.52 us -> 8.43 us  [on_device(): pairs = lax.all_gather(pair, 'tp', axis=1, tiled=True)]
    ppermute x0 -> x2, waiting for transfers between devices: none -> 4.5 us  [the longest x1 4.5 us: on_device(): lax.ppermute(jnp.where(edge, high, low), 'tp', [(0, 1), (1, 2), (2, 0), (...]
    ppermute x0 -> x2, starting transfers between devices: none -> 4.28 us  [the longest x1 3.61 us: on_device(): lax.ppermute(jnp.where(edge, high, low), 'tp', [(0, 1), (1, 2), (2, 0), (...]
    ppermute x2, waiting for transfers between devices: 0.01 us -> 3.75 us  [scattered(): far_arrived = lax.ppermute(far_other, 'tp', core_pairs)]
  transfers between devices with their start and end apart: 12 -> 13, of which waited for: 7 -> 7; matrix products, arithmetic and copies ran while one was open for 30% -> 26% of each run, Pallas kernels for 8% -> 4%
where the time goes in v3:
time: 314 us; the launch traced here: 310 us
  waiting for transfers between devices  124 us (39%)
  matrix products  89.2 us (28%)
  Pallas kernels  26.3 us (8%)
  blocking collectives  22.3 us (7%)
  other arithmetic  15.3 us (5%)
  between operations  14.6 us (5%)
  starting transfers between devices  10.7 us (3%)
  local copies, waits for them, and re-layouts  7.15 us (2%)
    ppermute x2, waiting for transfers between devices, shifted(): return lax.ppermute(value, axis, pairs)  71.9 us
    dot_general x12, matrix products, dot(): lax.dot_general(left, right, dims, preferred_element_type=jnp.float32)  57.3 us
    ppermute x2, waiting for transfers between devices, scattered(): across = lax.ppermute(far_sum, 'tp', far_pairs)  26.3 us
    dot_general x4, matrix products, out_term(): return jnp.dot(attended, block, preferred_element_type=jnp.float32)  21 us
    all_gather x1, blocking collectives, on_device(): row_dot = jnp.sum(lax.all_gather(row_dot, 'tp'), axis=0)  17.1 us
    pallas_call x1, Pallas kernels, attend_backward(): pl.pallas_call(backward_kernel, grid=(heads,), in_specs=[column, fixed, f...  13.3 us
    pallas_call x1, Pallas kernels, attend(): pl.pallas_call(attend_kernel, grid=(heads,), in_specs=[column, fixed, fix...  13 us
    dot_general x1, matrix products, on_device(): jnp.dot(normed_all, wq_dev, preferred_element_type=jnp.float32)  9.09 us
  transfers between devices with their start and end apart: 13, of which 7 were waited for; matrix products, arithmetic and copies ran while one was open for 26% of the time, Pallas kernels for 4%

profile of v3, /device:TPU:0, one launch (start us, length us, event | category | flops | bytes accessed | tf_op | source)
XLA Modules:
  0.0 309.6 jit_solution(9205779425610662756)
XLA Ops:
  7.2 0.0 copy-start
  7.2 0.0 all-gather.11.cloned.1.call-start
  7.2 3.0 collective-permute-start
  10.2 37.7 %collective-permute-done = bf16[1,768,1024]{2,1,0:T(8,128)(2,1)} collective-permute-done((bf16[1,768,1024]{2,1,0:T(8,128)(2,1)}, bf16[1,768,1024]{2,1,0:T(8,128)(2,1)}, u32[]{:S(2)}, u32[]{:S(2)}) %collective-permute-start) | collective-permute-done | bytes 1572896 | tf_op jit(solution)/shard_map/ppermute | solution.py:16
  48.0 0.0 all-gather.11.cloned.1.call-update
  48.0 0.0 all-gather.7.cloned.1.call-start
  48.0 1.8 collective-permute-start.1
  49.8 34.2 %collective-permute-done.1 = bf16[1,768,1024]{2,1,0:T(8,128)(2,1)} collective-permute-done((bf16[1,768,1024]{2,1,0:T(8,128)(2,1)}, bf16[1,768,1024]{2,1,0:T(8,128)(2,1)}, u32[]{:S(2)}, u32[]{:S(2)}) %collective-permute-start.1) | collective-permute-done | bytes 1572896 | tf_op jit(solution)/shard_map/ppermute | solution.py:16
  84.0 9.0 %all-gather.11.cloned.1.call-done = bf16[1,768,4096]{2,1,0:T(8,128)(2,1)} async-done(((bf16[1,768,1024]{2,1,0:T(8,128)(2,1)}), bf16[1,768,4096]{2,1,0:T(8,128)(2,1)}) %all-gather.11.cloned.1.call-update) | async-done | bytes 6291472 | tf_op jit(solution)/shard_map/all_gather | solution.py:153
  93.0 0.0 all-gather.7.cloned.1.call-update
  93.0 0.0 all-gather.9.cloned.1.call-start
  93.1 4.2 %fusion = f32[768]{0:T(1024)S(1)} fusion(bf16[768,4096]{1,0:T(8,128)(2,1)} %bitcast.99), kind=kLoop, calls=%fused_computation.2 | loop fusion | flops 9436416 | bytes 6294528 | tf_op jit(solution)/shard_map/reduce_sum | solution.py:158
  97.4 0.3 copy-done.11
  97.7 2.8 fusion.2
  100.5 0.0 copy-start.12
  100.5 1.8 fusion.61
  102.4 0.7 collective-permute-start.2
  103.0 3.6 %collective-permute-start.3 = (bf16[768,128]{1,0:T(8,128)(2,1)S(1)}, bf16[768,128]{1,0:T(8,128)(2,1)S(1)}, u32[]{:S(2)}, u32[]{:S(2)}) collective-permute-start(bf16[768,128]{1,0:T(8,128)(2,1)S(1)} %get-tuple-element.47), channel_id=1, source_target_pairs={{0,1},{1,2},{2,0},{3,3},{4,5},{5,6},{6,4},{7,7},{8,9},{9,10},{10,8... | collective-permute-start | bytes 589832 | tf_op jit(solution)/shard_map/ppermute | solution.py:163
  106.7 9.1 %fusion.49.q_ref = bf16[768,1024]{1,0:T(8,128)(2,1)S(1)} fusion(bf16[768,4096]{1,0:T(8,128)(2,1)S(1)} %fusion.2, bf16[1,4096,1024]{2,1,0:T(8,128)(2,1)} %param.8), kind=kOutput, calls=%fused_computation.58 | convolution fusion | flops 6443237376 | bytes 16252928 | tf_op jit(solution)/shard_map/dot_general | solution.py:169
  115.8 0.0 copy-start.1
  115.8 0.0 collective-permute-done.2
  115.8 4.5 %collective-permute-done.3 = bf16[768,128]{1,0:T(8,128)(2,1)S(1)} collective-permute-done((bf16[768,128]{1,0:T(8,128)(2,1)S(1)}, bf16[768,128]{1,0:T(8,128)(2,1)S(1)}, u32[]{:S(2)}, u32[]{:S(2)}) %collective-permute-start.3) | collective-permute-done | bytes 196640 | tf_op jit(solution)/shard_map/ppermute | solution.py:163
  120.3 13.0 %shard_map.109 = (bf16[768,1024]{1,0:T(8,128)(2,1)S(1)}, bf16[8,768,768]{2,1,0:T(8,128)(2,1)S(1)}) custom-call(bf16[768,1024]{1,0:T(8,128)(2,1)S(1)} %fusion.49.q_ref, bf16[768,128]{1,0:T(8,128)(2,1)S(1)} %get-tuple-element.46.k_ref, bf16[768,128]{1,0:T(8,128)(2,1)S(1)} %get-tuple-element.45.v_ref), custom_call_target="tpu_custom_call" | custom-call | flops 9663676416 | bytes 12582912 | tf_op jit(solution)/shard_map/pallas_call | solution.py:52
  133.4 3.6 %copy-done.10 = bf16[8,768,768]{2,1,0:T(8,128)(2,1)} copy-done((bf16[8,768,768]{2,1,0:T(8,128)(2,1)}, bf16[8,768,768]{2,1,0:T(8,128)(2,1)S(1)}, u32[]{:S(2)}) %copy-start.10) | copy-done | bytes 9437208
  137.0 5.1 %fusion.43 = bf16[768,1024]{1,0:T(8,128)(2,1)} fusion(bf16[768,1024]{1,0:T(8,128)(2,1)S(1)} %get-tuple-element.39.out_ref, bf16[1,1024,4096]{2,1,0:T(8,128)(2,1)} %param.10, s32[]{:T(128)S(6)} %select_n.74), kind=kOutput, calls=%fused_computation.56 | convolution fusion | flops 1611399168 | bytes 5242884 | tf_op jit(solution)/shard_map/dot_general | solution.py:177
  142.1 3.7 %collective-permute-done.4 = bf16[768,1024]{1,0:T(8,128)(2,1)} collective-permute-done((bf16[768,1024]{1,0:T(8,128)(2,1)}, bf16[768,1024]{1,0:T(8,128)(2,1)}, u32[]{:S(2)}, u32[]{:S(2)}) %collective-permute-start.4) | collective-permute-done | bytes 1572896 | tf_op jit(solution)/shard_map/ppermute | solution.py:133
  145.9 5.5 %add_convert_fusion.3 = bf16[768,1024]{1,0:T(8,128)(2,1)} fusion(bf16[768,1024]{1,0:T(8,128)(2,1)} %collective-permute-done.4, bf16[768,1024]{1,0:T(8,128)(2,1)} %copy-done.6, bf16[1,1024,4096]{2,1,0:T(8,128)(2,1)} %param.10, s32[]{:T(128)S(6)} %select_n.73), kind=kOutput, calls=%fused_computation.29 | convolution fusion | flops 1612972032 | bytes 6815748 | tf_op jit(solution)/shard_map/dot_general | solution.py:177
  151.3 11.1 %fusion.52.dout_ref = bf16[768,1024]{1,0:T(8,128)(2,1)S(1)} fusion(bf16[768,4096]{1,0:T(8,128)(2,1)} %all-gather.7.cloned.1.call-done, bf16[1,1024,4096]{2,1,0:T(8,128)(2,1)} %param.10), kind=kOutput, calls=%fused_computation.59 | convolution fusion | flops 6443237376 | bytes 16252928 | tf_op jit(solution)/shard_map/dot_general | solution.py:25
  162.5 13.3 %shard_map.110 = (bf16[768,1024]{1,0:T(8,128)(2,1)S(1)}, f32[768,128]{1,0:T(8,128)S(1)}, f32[768,128]{1,0:T(8,128)S(1)}) custom-call(bf16[768,1024]{1,0:T(8,128)(2,1)S(1)} %copy-done.2, bf16[768,128]{1,0:T(8,128)(2,1)S(1)} %get-tuple-element.46.k_ref, bf16[768,128]{1,0:T(8,128)(2,1)S(1)} %get-tuple-element.45.v_ref, bf16[768,1024]{1,0:T(8,128)(2,1)S(1)} %copy-done.7, ...), custom_call_target="tpu_custom_call" | custom-call | flops 12079595520 | bytes 15728640 | tf_op jit(solution)/shard_map/pallas_call | solution.py:101
  175.8 1.2 copy-done.4
  177.1 0.8 pad_maximum_fusion
  177.9 0.0 all-gather.9.cloned.1.call-update
  177.9 11.5 %convolution_convert_fusion = bf16[4096,1024]{1,0:T(8,128)(2,1)} fusion(bf16[768,4096]{1,0:T(8,128)(2,1)} %copy-done.12, bf16[768,1024]{1,0:T(8,128)(2,1)} %copy-done.4), kind=kOutput, calls=%fused_computation.10 | convolution fusion | flops 6446645248 | bytes 16252928 | tf_op jit(solution)/shard_map/dot_general | solution.py:25
  189.5 8.4 %all-gather.9.cloned.1.call-done = bf16[768,1024]{1,0:T(8,128)(2,1)} async-done(((bf16[768,256]{1,0:T(8,128)(2,1)}), bf16[768,1024]{1,0:T(8,128)(2,1)}) %all-gather.9.cloned.1.call-update) | async-done | bytes 1572880 | tf_op jit(solution)/shard_map/all_gather | solution.py:188
  197.9 1.1 constant_dynamic-slice_fusion.2
  199.0 3.9 %fusion.21 = f32[768,1024]{1,0:T(8,128)S(1)} fusion(bf16[768,1024]{1,0:T(8,128)(2,1)} %copy-done.4, bf16[1,4096,1024]{2,1,0:T(8,128)(2,1)} %param.8, s32[]{:T(128)S(6)} %select_n.74), kind=kOutput, calls=%fused_computation.34 | convolution fusion | flops 1610612736 | bytes 6815748 | tf_op jit(solution)/shard_map/dot_general | solution.py:25
  202.9 1.8 add_convert_fusion.2
  204.7 0.3 collective-permute-start.7
  205.0 5.2 %fusion.46 = bf16[768,1024]{1,0:T(8,128)(2,1)} fusion(bf16[768,1024]{1,0:T(8,128)(2,1)} %copy-done.6, bf16[1,1024,4096]{2,1,0:T(8,128)(2,1)} %param.10, s32[]{:T(128)S(6)} %select_n.76), kind=kOutput, calls=%fused_computation.57 | convolution fusion | flops 1611399168 | bytes 5242884 | tf_op jit(solution)/shard_map/dot_general | solution.py:177
  210.2 0.3 collective-permute-start.5
  210.4 0.3 collective-permute-start.6
  210.7 5.3 %fusion.27 = f32[768,1024]{1,0:T(8,128)} fusion(bf16[768,1024]{1,0:T(8,128)(2,1)S(1)} %copy-done.8, bf16[1,1024,4096]{2,1,0:T(8,128)(2,1)} %param.10, s32[]{:T(128)S(6)} %select_n.75), kind=kOutput, calls=%fused_computation.40 | convolution fusion | flops 1610612736 | bytes 6815748 | tf_op jit(solution)/shard_map/dot_general | solution.py:177
  216.0 0.2 multiply_reduce_fusion.1
  216.2 1.8 fusion.23
  218.1 0.0 copy-start.3
  218.1 0.0 collective-permute-done.7
  218.1 3.3 %add_convert_fusion.1 = bf16[768,1024]{1,0:T(8,128)(2,1)} fusion(bf16[768,1024]{1,0:T(8,128)(2,1)} %collective-permute-done.7, f32[768,1024]{1,0:T(8,128)S(1)} %fusion.23, bf16[768,256]{1,0:T(8,128)(2,1)S(1)} %pad_maximum_fusion.1, bf16[1,4096,256]{2,1,0:T(8,128)(2,1)S(1)} %copy-done, s32[]{:T(128)S(6)} %select_n.73), kind=kOutput, calls=%fused_computation.27 | convolution fusion | flops 405798912 | bytes 7208964 | tf_op jit(solution)/shard_map/dot_general | solution.py:25
  221.4 0.5 multiply_reduce_fusion
  221.9 0.0 slice-start.1
  221.9 3.5 %fusion.19 = f32[768,1024]{1,0:T(8,128)} fusion(bf16[768,1024]{1,0:T(8,128)(2,1)S(1)} %copy-done.5, bf16[1,4096,1024]{2,1,0:T(8,128)(2,1)S(1)} %bitcast.107, s32[]{:T(128)S(6)} %select_n.75), kind=kOutput, calls=%fused_computation.32 | convolution fusion | flops 1610612736 | bytes 6815748 | tf_op jit(solution)/shard_map/dot_general | solution.py:25
  225.5 2.3 fusion.64
  227.8 3.3 %fusion.7 = bf16[1,4096,256]{2,1,0:T(8,128)(2,1)} fusion(bf16[768,4096]{1,0:T(8,128)(2,1)S(1)} %bitcast.102, bf16[768,256]{1,0:T(8,128)(2,1)S(1)} %pad_maximum_fusion.1), kind=kOutput, calls=%fused_computation.12 | convolution fusion | flops 1611661312 | bytes 8781824 | tf_op jit(solution)/shard_map/dot_general | solution.py:25
  231.1 17.1 %all-gather.2 = f32[4,1,768]{2,1,0:T(1,128)S(1)} all-gather(f32[1,1,768]{2,1,0:T(1,128)S(1)} %reshape.52), channel_id=3, replica_groups=mesh['section'=8,'tp'=4] {'tp'}, dimensions={0}, use_global_device_ids=true | all-gather | bytes 15360 | tf_op jit(solution)/shard_map/all_gather | solution.py:219
  248.3 5.0 %add_convert_fusion = bf16[768,1024]{1,0:T(8,128)(2,1)S(1)} fusion(f32[768,1024]{1,0:T(8,128)} %fusion.64, bf16[768,1024]{1,0:T(8,128)(2,1)} %copy-done.4, bf16[1,4096,1024]{2,1,0:T(8,128)(2,1)} %param.8, s32[]{:T(128)S(6)} %select_n.76), kind=kOutput, calls=%fused_computation.26 | convolution fusion | flops 1612185600 | bytes 8388612 | tf_op jit(solution)/shard_map/dot_general | solution.py:25
  253.3 0.0 copy-start.9
  253.3 0.4 collective-permute-start.8
  253.6 0.3 collective-permute-start.9
  254.0 0.6 fusion.66
  254.6 0.2 copy-done.9
  254.7 9.1 %convert_bitcast_fusion = bf16[1,1024,4096]{2,1,0:T(8,128)(2,1)} fusion(bf16[768,1024]{1,0:T(8,128)(2,1)S(1)} %copy-done.9, bf16[768,4096]{1,0:T(8,128)(2,1)S(1)} %bitcast.109), kind=kOutput, calls=%fused_computation.9 | convolution fusion | flops 6446645248 | bytes 16252928 | tf_op jit(solution)/shard_map/dot_general | solution.py:25
  263.8 26.3 %collective-permute-done.9 = bf16[768,1024]{1,0:T(8,128)(2,1)S(1)} collective-permute-done((bf16[768,1024]{1,0:T(8,128)(2,1)S(1)}, bf16[768,1024]{1,0:T(8,128)(2,1)S(1)}, u32[]{:S(2)}, u32[]{:S(2)}) %collective-permute-start.9) | collective-permute-done | bytes 1572896 | tf_op jit(solution)/shard_map/ppermute | solution.py:137
  290.2 6.7 %fusion.14 = (f32[1024]{0:T(1024)S(1)}, bf16[1,768,1024]{2,1,0:T(8,128)(2,1)}, bf16[1,768,1024]{2,1,0:T(8,128)(2,1)}) fusion(bf16[1,768,1024]{2,1,0:T(8,128)(2,1)} %collective-permute-done, f32[768]{0:T(1024)S(1)} %add_rsqrt_fusion, bf16[768,1024]{1,0:T(8,128)(2,1)S(1)} %collective-permute-done.9, bf16[768,1024]{1,0:T(8,128)(2,1)S(1)} %collective-permute-done.8, ...), kind=kLoop, calls=%fused_computation.21 | loop fusion | flops 17300480 | bytes 22034432 | tf_op jit(solution)/shard_map/reduce_sum | solution.py:224
  296.8 5.2 %all_gather.20 = f32[4096]{0:T(1024)S(1)} all-gather(f32[1024]{0:T(1024)S(1)} %get-tuple-element.40), channel_id=1, replica_groups=mesh['section'=8,'tp'=4] {'tp'}, dimensions={0}, use_global_device_ids=true | all-gather | bytes 20480 | tf_op jit(solution)/shard_map/all_gather | solution.py:224
  302.0 0.6 copy.13
  (55 shorter events, 0.3 us)
Async XLA Ops:
  7.2 93.3 %copy-start = (bf16[1,4096,256]{2,1,0:T(8,128)(2,1)S(1)}, bf16[1,4096,256]{2,1,0:T(8,128)(2,1)}, u32[]{:S(2)}) copy-start(bf16[1,4096,256]{2,1,0:T(8,128)(2,1)} %param.9) | copy-start | bytes 6291460
  7.2 85.8 %all-gather.11.cloned.1.call-start = ((), (), s32[]{:S(2)}) async-start(), calls=%async_computation.2 | async-start | bytes 7864320 | tf_op jit(solution)/shard_map/all_gather | solution.py:153
  7.2 40.7 %collective-permute-start = (bf16[1,768,1024]{2,1,0:T(8,128)(2,1)}, bf16[1,768,1024]{2,1,0:T(8,128)(2,1)}, u32[]{:S(2)}, u32[]{:S(2)}) collective-permute-start(bf16[1,768,1024]{2,1,0:T(8,128)(2,1)} %param.6), channel_id=1, source_target_pairs={{0,4},{4,8},{8,12},{12,16},{16,20},{20,24},{24,28},{28,0},{1,5},{5... | collective-permute-start | bytes 4718600 | tf_op jit(solution)/shard_map/ppermute | solution.py:16
  48.0 103.3 %all-gather.7.cloned.1.call-start = ((), (), s32[]{:S(2)}) async-start(), calls=%async_computation | async-start | bytes 7864320 | tf_op jit(solution)/shard_map/all_gather | solution.py:172
  48.0 35.9 %collective-permute-start.1 = (bf16[1,768,1024]{2,1,0:T(8,128)(2,1)}, bf16[1,768,1024]{2,1,0:T(8,128)(2,1)}, u32[]{:S(2)}, u32[]{:S(2)}) collective-permute-start(bf16[1,768,1024]{2,1,0:T(8,128)(2,1)} %param.7), channel_id=1, source_target_pairs={{0,28},{4,0},{8,4},{12,8},{16,12},{20,16},{24,20},{28,24},{1,29},{... | collective-permute-start | bytes 4718600 | tf_op jit(solution)/shard_map/ppermute | solution.py:16
  93.0 4.4 %copy-start.16 = (f32[1,4096]{1,0:T(1,128)S(1)}, f32[1,4096]{1,0:T(1,128)}, u32[]{:S(2)}) copy-start(f32[1,4096]{1,0:T(1,128)} %param.11) | copy-start | bytes 49156
  93.0 104.9 %all-gather.9.cloned.1.call-start = ((), (), s32[]{:S(2)}) async-start(), calls=%async_computation.1 | async-start | bytes 1966080 | tf_op jit(solution)/shard_map/all_gather | solution.py:188
  93.1 4.6 %copy-start.11 = (bf16[1,768,4096]{2,1,0:T(8,128)(2,1)S(1)}, bf16[1,768,4096]{2,1,0:T(8,128)(2,1)}, u32[]{:S(2)}) copy-start(bf16[1,768,4096]{2,1,0:T(8,128)(2,1)} %all-gather.11.cloned.1.call-done) | copy-start | bytes 18874372
  100.5 6.2 %copy-start.12 = (bf16[768,4096]{1,0:T(8,128)(2,1)}, bf16[768,4096]{1,0:T(8,128)(2,1)S(1)}, u32[]{:S(2)}) copy-start(bf16[768,4096]{1,0:T(8,128)(2,1)S(1)} %fusion.2) | copy-start | bytes 18874372
  102.4 13.4 %collective-permute-start.2 = (bf16[768,128]{1,0:T(8,128)(2,1)S(1)}, bf16[768,128]{1,0:T(8,128)(2,1)S(1)}, u32[]{:S(2)}, u32[]{:S(2)}) collective-permute-start(bf16[768,128]{1,0:T(8,128)(2,1)S(1)} %get-tuple-element.48), channel_id=1, source_target_pairs={{0,0},{1,3},{2,1},{3,2},{4,4},{5,7},{6,5},{7,6},{8,8},{9,11},{10,9... | collective-permute-start | bytes 589832 | tf_op jit(solution)/shard_map/ppermute | solution.py:166
  103.0 17.2 %collective-permute-start.3 = (bf16[768,128]{1,0:T(8,128)(2,1)S(1)}, bf16[768,128]{1,0:T(8,128)(2,1)S(1)}, u32[]{:S(2)}, u32[]{:S(2)}) collective-permute-start(bf16[768,128]{1,0:T(8,128)(2,1)S(1)} %get-tuple-element.47), channel_id=1, source_target_pairs={{0,1},{1,2},{2,0},{3,3},{4,5},{5,6},{6,4},{7,7},{8,9},{9,10},{10,8... | collective-permute-start | bytes 589832 | tf_op jit(solution)/shard_map/ppermute | solution.py:163
  115.8 17.6 %copy-start.1 = (bf16[768,1024]{1,0:T(8,128)(2,1)}, bf16[768,1024]{1,0:T(8,128)(2,1)S(1)}, u32[]{:S(2)}) copy-start(bf16[768,1024]{1,0:T(8,128)(2,1)S(1)} %fusion.49.q_ref) | copy-start | bytes 4718596
  133.4 3.6 %copy-start.10 = (bf16[8,768,768]{2,1,0:T(8,128)(2,1)}, bf16[8,768,768]{2,1,0:T(8,128)(2,1)S(1)}, u32[]{:S(2)}) copy-start(bf16[8,768,768]{2,1,0:T(8,128)(2,1)S(1)} %get-tuple-element.28.probs_ref) | copy-start | bytes 28311556
  137.0 5.1 %copy-start.6 = (bf16[768,1024]{1,0:T(8,128)(2,1)}, bf16[768,1024]{1,0:T(8,128)(2,1)S(1)}, u32[]{:S(2)}) copy-start(bf16[768,1024]{1,0:T(8,128)(2,1)S(1)} %get-tuple-element.39.out_ref) | copy-start | bytes 4718596
  142.1 3.8 %collective-permute-start.4 = (bf16[768,1024]{1,0:T(8,128)(2,1)}, bf16[768,1024]{1,0:T(8,128)(2,1)}, u32[]{:S(2)}, u32[]{:S(2)}) collective-permute-start(bf16[768,1024]{1,0:T(8,128)(2,1)} %fusion.43), channel_id=1, source_target_pairs={{0,1},{1,0},{2,3},{3,2},{4,5},{5,4},{6,7},{7,6},{8,9},{9,8},{10,11... | collective-permute-start | bytes 4718600 | tf_op jit(solution)/shard_map/ppermute | solution.py:133
  151.3 11.1 %copy-start.2 = (bf16[768,1024]{1,0:T(8,128)(2,1)S(1)}, bf16[768,1024]{1,0:T(8,128)(2,1)}, u32[]{:S(2)}) copy-start(bf16[768,1024]{1,0:T(8,128)(2,1)} %copy-done.1) | copy-start | bytes 4718596
  151.3 11.1 %copy-start.7 = (bf16[768,1024]{1,0:T(8,128)(2,1)S(1)}, bf16[768,1024]{1,0:T(8,128)(2,1)}, u32[]{:S(2)}) copy-start(bf16[768,1024]{1,0:T(8,128)(2,1)} %copy-done.6) | copy-start | bytes 4718596
  175.8 1.3 copy-start.4
  204.7 13.4 %collective-permute-start.7 = (bf16[768,1024]{1,0:T(8,128)(2,1)}, bf16[768,1024]{1,0:T(8,128)(2,1)}, u32[]{:S(2)}, u32[]{:S(2)}) collective-permute-start(bf16[768,1024]{1,0:T(8,128)(2,1)} %add_convert_fusion.2), channel_id=1, source_target_pairs={{0,1},{1,0},{2,3},{3,2},{4,5},{5,4},{6,7},{7,6},{8,9},{9,8},{10,11... | collective-permute-start | bytes 4718600 | tf_op jit(solution)/shard_map/ppermute | solution.py:133
  205.0 5.7 %copy-start.8 = (bf16[768,1024]{1,0:T(8,128)(2,1)S(1)}, bf16[768,1024]{1,0:T(8,128)(2,1)}, u32[]{:S(2)}) copy-start(bf16[768,1024]{1,0:T(8,128)(2,1)} %copy-done.6) | copy-start | bytes 4718596
  205.0 11.2 %slice-start.2 = ((s8[8388608]{0:T(1024)(128)(4,1)}), s8[4194304]{0:T(1024)(128)(4,1)S(1)}, s32[]{:S(2)}) async-start(s8[8388608]{0:T(1024)(128)(4,1)} %bitcast.106), calls=%async_computation.5 | async-start | bytes 8388608
  210.2 6.0 %copy-start.5 = (bf16[768,1024]{1,0:T(8,128)(2,1)S(1)}, bf16[768,1024]{1,0:T(8,128)(2,1)}, u32[]{:S(2)}) copy-start(bf16[768,1024]{1,0:T(8,128)(2,1)} %copy-done.4) | copy-start | bytes 4718596
  210.2 6.1 %slice-start.3 = ((s8[8388608]{0:T(1024)(128)(4,1)}), s8[4194304]{0:T(1024)(128)(4,1)S(1)}, s32[]{:S(2)}) async-start(s8[8388608]{0:T(1024)(128)(4,1)} %bitcast.106), calls=%async_computation.6 | async-start | bytes 8388608
  210.2 53.7 %collective-permute-start.5 = (bf16[768,1024]{1,0:T(8,128)(2,1)}, bf16[768,1024]{1,0:T(8,128)(2,1)}, u32[]{:S(2)}, u32[]{:S(2)}) collective-permute-start(bf16[768,1024]{1,0:T(8,128)(2,1)} %fusion.46), channel_id=1, source_target_pairs={{0,1},{1,0},{2,3},{3,2},{4,5},{5,4},{6,7},{7,6},{8,9},{9,8},{10,11... | collective-permute-start | bytes 4718600 | tf_op jit(solution)/shard_map/ppermute | solution.py:139
  210.4 53.4 %collective-permute-start.6 = (bf16[768,1024]{1,0:T(8,128)(2,1)}, bf16[768,1024]{1,0:T(8,128)(2,1)}, u32[]{:S(2)}, u32[]{:S(2)}) collective-permute-start(bf16[768,1024]{1,0:T(8,128)(2,1)} %add_convert_fusion.3), channel_id=1, source_target_pairs={{0,2},{1,3},{2,0},{3,1},{4,6},{5,7},{6,4},{7,5},{8,10},{9,11},{10,... | collective-permute-start | bytes 4718600 | tf_op jit(solution)/shard_map/ppermute | solution.py:137
  218.1 3.4 %copy-start.3 = (bf16[768,1024]{1,0:T(8,128)(2,1)S(1)}, bf16[768,1024]{1,0:T(8,128)(2,1)}, u32[]{:S(2)}) copy-start(bf16[768,1024]{1,0:T(8,128)(2,1)} %copy-done.1) | copy-start | bytes 4718596
  221.4 6.3 %slice-start = ((s8[6291456]{0:T(1024)(128)(4,1)}), s8[4194304]{0:T(1024)(128)(4,1)S(1)}, s32[]{:S(2)}) async-start(s8[6291456]{0:T(1024)(128)(4,1)} %bitcast.101), calls=%async_computation.3 | async-start | bytes 8388608
  221.9 5.9 %slice-start.1 = ((s8[6291456]{0:T(1024)(128)(4,1)}), s8[2097152]{0:T(1024)(128)(4,1)S(1)}, s32[]{:S(2)}) async-start(s8[6291456]{0:T(1024)(128)(4,1)} %bitcast.101), calls=%async_computation.4 | async-start | bytes 4194304
  248.2 6.4 %slice-start.4 = ((s8[6291456]{0:T(1024)(128)(4,1)}), s8[4194304]{0:T(1024)(128)(4,1)S(1)}, s32[]{:S(2)}) async-start(s8[6291456]{0:T(1024)(128)(4,1)} %bitcast.108), calls=%async_computation.7 | async-start | bytes 8388608
  248.2 5.4 %copy-start.15 = (bf16[768,1024]{1,0:T(8,128)(2,1)S(1)}, bf16[768,1024]{1,0:T(8,128)(2,1)}, u32[]{:S(2)}) copy-start(bf16[768,1024]{1,0:T(8,128)(2,1)} %add_convert_fusion.1) | copy-start | bytes 4718596
  248.2 6.3 %slice-start.5 = ((s8[6291456]{0:T(1024)(128)(4,1)}), s8[2097152]{0:T(1024)(128)(4,1)S(1)}, s32[]{:S(2)}) async-start(s8[6291456]{0:T(1024)(128)(4,1)} %bitcast.108), calls=%async_computation.8 | async-start | bytes 4194304
  253.3 1.5 copy-start.9
  253.3 10.6 %collective-permute-start.8 = (bf16[768,1024]{1,0:T(8,128)(2,1)S(1)}, bf16[768,1024]{1,0:T(8,128)(2,1)S(1)}, u32[]{:S(2)}, u32[]{:S(2)}) collective-permute-start(bf16[768,1024]{1,0:T(8,128)(2,1)S(1)} %add_convert_fusion), channel_id=1, source_target_pairs={{0,1},{1,0},{2,3},{3,2},{4,5},{5,4},{6,7},{7,6},{8,9},{9,8},{10,11... | collective-permute-start | bytes 4718600 | tf_op jit(solution)/shard_map/ppermute | solution.py:139
  253.6 36.5 %collective-permute-start.9 = (bf16[768,1024]{1,0:T(8,128)(2,1)S(1)}, bf16[768,1024]{1,0:T(8,128)(2,1)S(1)}, u32[]{:S(2)}, u32[]{:S(2)}) collective-permute-start(bf16[768,1024]{1,0:T(8,128)(2,1)S(1)} %copy-done.15), channel_id=1, source_target_pairs={{0,2},{1,3},{2,0},{3,1},{4,6},{5,7},{6,4},{7,5},{8,10},{9,11},{10,... | collective-permute-start | bytes 4718600 | tf_op jit(solution)/shard_map/ppermute | solution.py:137
  254.7 35.4 %copy-start.13 = (f32[768,1024]{1,0:T(8,128)S(1)}, f32[768,1024]{1,0:T(8,128)}, u32[]{:S(2)}) copy-start(f32[768,1024]{1,0:T(8,128)} %fusion.27) | copy-start | bytes 9437188
  254.7 35.4 %copy-start.14 = (f32[768,1024]{1,0:T(8,128)S(1)}, f32[768,1024]{1,0:T(8,128)}, u32[]{:S(2)}) copy-start(f32[768,1024]{1,0:T(8,128)} %fusion.19) | copy-start | bytes 9437188
Sparse Core Ops, SparseCore 0:
  48.1 44.8 all-gather.10
  94.6 51.3 all-gather.6
  178.0 19.8 all-gather.8
